TPU v7x, 128 devices: a whole 4x4x4 slice. The times are simulated.
128 devices in a mesh: req: 64 (over z, x, y), kv: 2 (over core).
Axes of the slice: x: 4, y: 4, z: 4, core: 2. Of those that a mesh axis runs over, the one named last changes fastest.
Arguments:
- tokens: bfloat16 [1024, 1536], P('req'), may hold values from -6 to 6
- gain_attn: bfloat16 [1536], replicated, may hold values from 0.099609375 to 1.8984375
- w_query: bfloat16 [1536, 1536], P(None, 'kv'), may hold values from -0.15625 to 0.15625
- w_key: bfloat16 [1536, 256], P(None, 'kv'), may hold values from -0.15625 to 0.15625
- w_value: bfloat16 [1536, 256], P(None, 'kv'), may hold values from -0.15625 to 0.15625
- w_out: bfloat16 [1536, 1536], P('kv'), may hold values from -0.15625 to 0.15625
- cache_k: bfloat16 [4096, 128, 256], P('req', None, 'kv'), may hold values from -720 to 720
- cache_v: bfloat16 [4096, 128, 256], P('req', None, 'kv'), may hold values from -6 to 6
- page_table: int32 [1024, 4], P('req'), may hold values from 0 to 63, as said below
- lengths: int32 [1024], replicated, may hold values from 1 to 512, as said below
- new_owner: int32 [64], replicated, may hold values from 0 to 63, as said below
- gain_moe: bfloat16 [1536], replicated, may hold values from 0.099609375 to 1.8984375
- w_router: bfloat16 [1536, 32], replicated, may hold values from -0.15625 to 0.15625
- routes: int32 [1024, 4], P(('req', 'kv')), may hold values from 0 to 31, all different within a row; in each aligned block of 8 rows (0 to 7, 8 to 15, ...) at most 2 rows name the same one
- w_gate: bfloat16 [64, 1536, 384], P('req', None, 'kv'), may hold values from -0.15625 to 0.15625
- w_up: bfloat16 [64, 1536, 384], P('req', None, 'kv'), may hold values from -0.15625 to 0.15625
- w_down: bfloat16 [64, 1536, 384], P('req', None, 'kv'), may hold values from -0.21875 to 0.21875
Outputs:
- layer_out: bfloat16 [1024, 1536], P(('req', 'kv'))
Inputs may be any that keep to these rules, and one draw needn't show every extreme that they name: `lengths`: the last slot of each device (15, 31, ...) holds at most 256, and some last slot holds exactly 256; some length equals 512. `page_table`: the page indices of the 16 slots of one device are together a permutation of 0 to 63. `new_owner`: A permutation of the devices of req. `routes`: in each aligned block of 8 rows (the rows of one device) no expert is named by more than 2 rows.
All inputs are finite; a program needn't handle non-finite values.
Results may differ from a plain program's by a relative error of at most 0.015.
The roundings to bfloat16 on the way count: a program that leaves them out, or rounds other values in their place, can miss the bound.
Values may be sent and summed in bfloat16 or wider, within the bound.
A program may use at most 128 MiB of HBM per device.

v0:
```python
import jax
import jax.numpy as jnp
from jax import lax
from jax.sharding import PartitionSpec as P

MOVE_LEN = 256


def rms_scaled(values, gain_vec):
    wide = values.astype(jnp.float32)
    squares = jnp.mean(wide * wide, axis=-1, keepdims=True)
    return (wide * lax.rsqrt(squares + 1e-06) * gain_vec.astype(jnp.float32)).astype(jnp.bfloat16)


def cache_partial(queries, page_keys, page_values, live_len):
    inv_root = queries.shape[-1] ** (-0.5)
    scores = (
        jnp.einsum("rgd,rtd->rgt", queries, page_keys, preferred_element_type=jnp.float32)
        * inv_root
    )
    positions = lax.broadcasted_iota(jnp.int32, scores.shape, 2)
    live_mask = positions < live_len[:, None, None]
    scores = jnp.where(live_mask, scores, -1e30)
    top_score = jnp.max(scores, axis=-1)
    weights = jnp.where(live_mask, jnp.exp(scores - top_score[..., None]), 0.0)
    totals = jnp.sum(weights, axis=-1)
    accumulated = jnp.einsum(
        "rgt,rtd->rgd",
        weights.astype(jnp.bfloat16),
        page_values,
        preferred_element_type=jnp.float32,
    )
    return (accumulated, top_score, totals)


def finish_heads(accumulated, top_score, totals, queries, key_now, value_now):
    inv_root = queries.shape[-1] ** (-0.5)
    own_score = (
        jnp.einsum("rgd,rd->rg", queries, key_now, preferred_element_type=jnp.float32) * inv_root
    )
    joint_max = jnp.maximum(top_score, own_score)
    old_part = jnp.exp(top_score - joint_max)
    new_part = jnp.exp(own_score - joint_max)
    merged = (
        accumulated * old_part[..., None]
        + new_part[..., None] * value_now.astype(jnp.float32)[:, None, :]
    )
    result = merged / (totals * old_part + new_part)[..., None]
    return result.astype(jnp.bfloat16).reshape(queries.shape[0], -1)


def shards(
    tokens,
    gain_attn,
    w_query,
    w_key,
    w_value,
    w_out,
    cache_k,
    cache_v,
    page_table,
    lengths,
    new_owner,
    gain_moe,
    w_router,
    routes,
    w_gate,
    w_up,
    w_down,
):
    req_dev = tokens.shape[0]
    half_rows = req_dev // 2
    req_count = lax.axis_size("req")
    req_index = lax.axis_index("req")
    kv_index = lax.axis_index("kv")
    last_slot = req_dev - 1
    normed = rms_scaled(tokens, gain_attn)
    head_dim = w_key.shape[1]
    groups = w_query.shape[1] // head_dim
    queries = (
        jnp.dot(normed, w_query, preferred_element_type=jnp.float32)
        .astype(jnp.bfloat16)
        .reshape(req_dev, groups, head_dim)
    )
    key_now = jnp.dot(normed, w_key, preferred_element_type=jnp.float32).astype(jnp.bfloat16)
    value_now = jnp.dot(normed, w_value, preferred_element_type=jnp.float32).astype(jnp.bfloat16)
    own_len = lax.dynamic_slice_in_dim(lengths, req_index * req_dev, req_dev)
    page_keys = cache_k[page_table].reshape(req_dev, -1, head_dim)
    page_values = cache_v[page_table].reshape(req_dev, -1, head_dim)
    peer_ids = jnp.arange(req_count, dtype=jnp.int32)
    target = new_owner[req_index]
    source = jnp.sum(jnp.where(new_owner == req_index, peer_ids, 0))
    empty_bf = jnp.zeros((), jnp.bfloat16)
    chosen = (peer_ids == target)[:, None, None]
    outgoing_k = jnp.where(chosen, page_keys[last_slot, :MOVE_LEN][None], empty_bf)
    outgoing_v = jnp.where(chosen, page_values[last_slot, :MOVE_LEN][None], empty_bf)
    arrived_k, arrived_v = (
        lax.all_to_all(outgoing_k, "req", split_axis=0, concat_axis=0, tiled=True),
        lax.all_to_all(outgoing_v, "req", split_axis=0, concat_axis=0, tiled=True),
    )
    page_keys = page_keys.at[last_slot, :MOVE_LEN].set(arrived_k[source])
    page_values = page_values.at[last_slot, :MOVE_LEN].set(arrived_v[source])
    live_len = own_len.at[last_slot].set(lengths[source * req_dev + last_slot])
    accumulated, top_score, totals = cache_partial(queries, page_keys, page_values, live_len)
    attended = finish_heads(accumulated, top_score, totals, queries, key_now, value_now)
    head_terms = jnp.dot(attended, w_out, preferred_element_type=jnp.float32)
    head_total = lax.psum_scatter(head_terms, "kv", scatter_dimension=0, tiled=True)
    residual = lax.dynamic_slice_in_dim(tokens, kv_index * half_rows, half_rows, 0)
    middle = (residual.astype(jnp.float32) + head_total).astype(jnp.bfloat16)
    normed_two = rms_scaled(middle, gain_moe)
    logits = jnp.dot(normed_two, w_router, preferred_element_type=jnp.float32)
    route_weight = jax.nn.softmax(jnp.take_along_axis(logits, routes, axis=1), axis=-1)
    experts = req_count // 2
    topk = routes.shape[1]
    capacity = max(2, half_rows * topk // experts)
    flat_routes = routes.reshape(-1)
    onehot = (flat_routes[:, None] == jnp.arange(experts, dtype=jnp.int32)[None, :]).astype(
        jnp.int32
    )
    slot_rank = jnp.sum((jnp.cumsum(onehot, axis=0) - onehot) * onehot, axis=1)
    expert_of_peer = peer_ids // 2
    slot_ids = jnp.arange(capacity, dtype=jnp.int32)
    placement_map = (flat_routes[None, None, :] == expert_of_peer[:, None, None]) & (
        slot_rank[None, None, :] == slot_ids[None, :, None]
    )
    placement_map = placement_map.astype(jnp.float32).reshape(req_count, capacity, half_rows, topk)
    picked = jnp.sum(placement_map, axis=-1)
    blending = jnp.sum(placement_map * route_weight[None, None], axis=-1)
    outgoing = jnp.einsum(
        "pci,id->pcd", picked.astype(jnp.bfloat16), normed_two, preferred_element_type=jnp.float32
    ).astype(jnp.bfloat16)
    gate_half, up_half, down_half = (
        lax.all_gather(w_gate, "kv", axis=2, tiled=True),
        lax.all_gather(w_up, "kv", axis=2, tiled=True),
        lax.all_gather(w_down, "kv", axis=2, tiled=True),
    )
    received = lax.all_to_all(outgoing, "req", split_axis=0, concat_axis=0, tiled=True)
    senders, slot_count, feature_count = received.shape
    flat_rows = received.reshape(senders * slot_count, feature_count)
    gate_val = jnp.dot(flat_rows, gate_half[0], preferred_element_type=jnp.float32)
    up_val = jnp.dot(flat_rows, up_half[0], preferred_element_type=jnp.float32)
    hidden = (jax.nn.relu(gate_val) * up_val).astype(jnp.bfloat16)
    result = lax.dot_general(
        hidden, down_half[0], (((1,), (1,)), ((), ())), preferred_element_type=jnp.float32
    )
    returned = lax.all_to_all(
        result.reshape(senders, slot_count, feature_count),
        "req",
        split_axis=0,
        concat_axis=0,
        tiled=True,
    )
    mixed = jnp.einsum("pci,pcd->id", blending, returned, precision=lax.Precision.HIGHEST)
    return (middle.astype(jnp.float32) + mixed).astype(jnp.bfloat16)


def solution(mesh):
    return jax.shard_map(
        shards,
        mesh=mesh,
        in_specs=(
            P("req", None),
            P(),
            P(None, "kv"),
            P(None, "kv"),
            P(None, "kv"),
            P("kv", None),
            P("req", None, "kv"),
            P("req", None, "kv"),
            P("req", None),
            P(),
            P(),
            P(),
            P(),
            P(("req", "kv"), None),
            P("req", None, "kv"),
            P("req", None, "kv"),
            P("req", None, "kv"),
        ),
        out_specs=P(("req", "kv"), None),
        check_vma=False,
    )
```

profile of v0, /device:TPU:1, one launch (start us, length us, event | category | flops | bytes accessed | tf_op | source)
XLA Modules:
  0.0 235.6 jit_solution(13709867377025384650)
XLA Ops:
  6.5 1.4 dynamic_slice.21
  7.9 0.6 iota_compare_fusion.3
  8.6 0.7 compare_select_fusion.1
  9.5 3.7 %gather_fusion = bf16[64,128,128]{2,1,0:T(8,128)(2,1)} fusion(bf16[64,128,128]{2,1,0:T(8,128)(2,1)} %param.29, s32[1024]{0:T(1024)S(1)} %pad_clamp_fusion), kind=kCustom, calls=%fused_computation | custom fusion | bytes 4194560 | tf_op jit(solution)/shard_map/gather | solution.py:88
  13.2 3.8 %gather_fusion.1 = bf16[64,128,128]{2,1,0:T(8,128)(2,1)} fusion(bf16[64,128,128]{2,1,0:T(8,128)(2,1)} %param.30, s32[1024]{0:T(1024)S(1)} %pad_clamp_fusion), kind=kCustom, calls=%fused_computation.1 | custom fusion | bytes 4194560 | tf_op jit(solution)/shard_map/gather | solution.py:89
  17.0 0.9 slice_bitcast_fusion
  17.8 2.6 %broadcast_select_fusion.1 = (bf16[64,256,128]{2,1,0:T(8,128)(2,1)S(1)}, bf16[64,256,128]{2,1,0:T(8,128)(2,1)}) fusion(pred[64]{0:T(512)(128)(4,1)S(1)} %iota_compare_fusion.3, bf16[256,128]{1,0:T(8,128)(2,1)S(1)} %get-tuple-element.53, bf16[256,128]{1,0:T(8,128)(2,1)S(1)} %get-tuple-element.52), kind=kLoop, calls=%fused_computation.4 | loop fusion | flops 4194304 | bytes 8519744 | tf_op jit(solution)/shard_map/jit(_where)/select_n | solution.py:95
  20.4 62.2 %all_to_all.20 = bf16[64,256,128]{2,1,0:T(8,128)(2,1)} all-to-all(bf16[64,256,128]{2,1,0:T(8,128)(2,1)S(1)} %get-tuple-element.48), channel_id=1, replica_groups=mesh['req'=64,'kv'=2] {'req'}, dimensions={0} | all-to-all | bytes 8388608 | tf_op jit(solution)/shard_map/all_to_all | solution.py:98
  82.6 6.5 %all-to-all-start.1 = ((bf16[64,256,128]{2,1,0:T(8,128)(2,1)}), bf16[64,256,128]{2,1,0:T(8,128)(2,1)}, u32[]{:S(2)}, u32[]{:S(2)}) async-start(bf16[64,256,128]{2,1,0:T(8,128)(2,1)} %get-tuple-element.49), calls=%async_computation.1 | async-start | bytes 8388608 | tf_op jit(solution)/shard_map/all_to_all | solution.py:99
  89.2 0.6 fusion.54
  92.0 2.1 convolution_convert_fusion.1
  94.8 0.8 dynamic_slice.19
  95.6 0.8 constant_dynamic-update-slice_fusion
  97.0 1.5 dynamic-slice_dynamic-update-slice_fusion.1
  98.5 2.3 fusion.62
  101.0 37.3 %all-to-all-done.1 = bf16[64,256,128]{2,1,0:T(8,128)(2,1)} async-done(((bf16[64,256,128]{2,1,0:T(8,128)(2,1)}), bf16[64,256,128]{2,1,0:T(8,128)(2,1)}, u32[]{:S(2)}, u32[]{:S(2)}) %all-to-all-start.1) | async-done | bytes 4194336 | tf_op jit(solution)/shard_map/all_to_all | solution.py:99
  138.4 1.5 dynamic-slice_dynamic-update-slice_fusion
  139.8 2.0 fusion.20
  141.9 1.1 fusion.39
  143.0 0.7 all-gather.6.cloned.1.call-update
  143.8 0.7 all-gather.4.cloned.1.call-update
  146.1 9.9 %reduce-scatter.2.cloned.1.call-done = f32[8,1536]{1,0:T(8,128)} async-done(((f32[16,1536]{1,0:T(8,128)}), f32[8,1536]{1,0:T(8,128)}) %reduce-scatter.2.cloned.1.call-update) | async-done | bytes 49168 | tf_op jit(solution)/shard_map/reduce_scatter | solution.py:107
  155.9 0.9 fusion.34
  157.1 0.7 gather_fusion.2
  159.2 21.0 %all_to_all.21 = bf16[64,2,1536]{2,1,0:T(2,128)(2,1)S(1)} all-to-all(bf16[64,2,1536]{2,1,0:T(2,128)(2,1)S(1)} %copy.70), channel_id=1, replica_groups=mesh['req'=64,'kv'=2] {'req'}, dimensions={0} | all-to-all | bytes 786432 | tf_op jit(solution)/shard_map/all_to_all | solution.py:137
  180.4 1.8 fusion.4
  182.2 3.7 %all-gather.4.cloned.1.call-done = bf16[1,1536,384]{1,2,0:T(8,128)(2,1)} async-done(((bf16[1,1536,192]{1,2,0:T(8,128)(2,1)}), bf16[1,1536,384]{1,2,0:T(8,128)(2,1)}) %all-gather.4.cloned.1.call-update) | async-done | bytes 1179664 | tf_op jit(solution)/shard_map/all_gather | solution.py:133
  185.8 1.8 fusion.15
  187.7 13.0 %all-gather.8.cloned.1.call-done = bf16[1,1536,384]{1,2,0:T(8,128)(2,1)} async-done(((bf16[1,1536,192]{1,2,0:T(8,128)(2,1)}), bf16[1,1536,384]{1,2,0:T(8,128)(2,1)}) %all-gather.8.cloned.1.call-update) | async-done | bytes 1179664 | tf_op jit(solution)/shard_map/all_gather | solution.py:135
  200.6 1.6 fusion.2
  202.9 25.0 %all_to_all.22 = f32[64,2,1536]{2,1,0:T(2,128)S(1)} all-to-all(f32[64,2,1536]{2,1,0:T(2,128)S(1)} %copy.73), channel_id=1, replica_groups=mesh['req'=64,'kv'=2] {'req'}, dimensions={0} | all-to-all | bytes 1572864 | tf_op jit(solution)/shard_map/all_to_all | solution.py:146
  227.9 1.2 fusion.1
  (66 shorter events, 5.3 us)
Async XLA Ops:
  6.5 135.3 %copy-start = (bf16[768,1536]{1,0:T(8,128)(2,1)S(1)}, bf16[768,1536]{1,0:T(8,128)(2,1)}, u32[]{:S(2)}) copy-start(bf16[768,1536]{1,0:T(8,128)(2,1)} %param.28) | copy-start | bytes 7077892
  82.6 6.6 %copy-start.8 = (s32[64]{0:T(128)S(1)}, s32[64]{0:T(128)}, u32[]{:S(2)}) copy-start(s32[64]{0:T(128)} %param.33) | copy-start | bytes 772
  82.6 9.2 %copy-start.5 = (bf16[1536]{0:T(1024)(128)(2,1)S(1)}, bf16[1536]{0:T(1024)(128)(2,1)}, u32[]{:S(2)}) copy-start(bf16[1536]{0:T(1024)(128)(2,1)} %param.24) | copy-start | bytes 9220
  82.6 9.2 %copy-start.1 = (bf16[16,1536]{1,0:T(8,128)(2,1)S(1)}, bf16[16,1536]{1,0:T(8,128)(2,1)}, u32[]{:S(2)}) copy-start(bf16[16,1536]{1,0:T(8,128)(2,1)} %param.23) | copy-start | bytes 147460
  82.6 55.8 %all-to-all-start.1 = ((bf16[64,256,128]{2,1,0:T(8,128)(2,1)}), bf16[64,256,128]{2,1,0:T(8,128)(2,1)}, u32[]{:S(2)}, u32[]{:S(2)}) async-start(bf16[64,256,128]{2,1,0:T(8,128)(2,1)} %get-tuple-element.49), calls=%async_computation.1 | async-start | bytes 8388608 | tf_op jit(solution)/shard_map/all_to_all | solution.py:99
  89.1 7.3 %copy-start.2 = (bf16[1536,128]{1,0:T(8,128)(2,1)S(1)}, bf16[1536,128]{1,0:T(8,128)(2,1)}, u32[]{:S(2)}) copy-start(bf16[1536,128]{1,0:T(8,128)(2,1)} %param.26) | copy-start | bytes 1179652
  89.1 7.6 %copy-start.3 = (bf16[1536,128]{1,0:T(8,128)(2,1)S(1)}, bf16[1536,128]{1,0:T(8,128)(2,1)}, u32[]{:S(2)}) copy-start(bf16[1536,128]{1,0:T(8,128)(2,1)} %param.27) | copy-start | bytes 1179652
  89.1 66.8 %reduce-scatter.2.cloned.1.call-start = ((), (), s32[]{:S(2)}) async-start(), calls=%async_computation.5 | async-start | bytes 147456 | tf_op jit(solution)/shard_map/reduce_scatter | solution.py:107
  141.9 3.2 %copy-start.4 = (s32[8,4]{0,1:T(4,128)S(1)}, s32[8,4]{0,1:T(4,128)}, u32[]{:S(2)}) copy-start(s32[8,4]{0,1:T(4,128)} %param.36) | copy-start | bytes 388
  141.9 3.4 %copy-start.6 = (bf16[1536]{0:T(1024)(128)(2,1)S(1)}, bf16[1536]{0:T(1024)(128)(2,1)}, u32[]{:S(2)}) copy-start(bf16[1536]{0:T(1024)(128)(2,1)} %param.34) | copy-start | bytes 9220
  141.9 15.0 %copy-start.7 = (bf16[1536,32]{0,1:T(8,128)(2,1)S(1)}, bf16[1536,32]{0,1:T(8,128)(2,1)}, u32[]{:S(2)}) copy-start(bf16[1536,32]{0,1:T(8,128)(2,1)} %param.35) | copy-start | bytes 294916
  143.0 37.4 %all-gather.6.cloned.1.call-start = ((), (), s32[]{:S(2)}) async-start(), calls=%async_computation.7 | async-start | bytes 1769472 | tf_op jit(solution)/shard_map/all_gather | solution.py:134
  143.7 42.1 %all-gather.4.cloned.1.call-start = ((), (), s32[]{:S(2)}) async-start(), calls=%async_computation.6 | async-start | bytes 1769472 | tf_op jit(solution)/shard_map/all_gather | solution.py:133
  144.5 56.2 %all-gather.8.cloned.1.call-start = ((), (), s32[]{:S(2)}) async-start(), calls=%async_computation.8 | async-start | bytes 1769472 | tf_op jit(solution)/shard_map/all_gather | solution.py:135
Sparse Core Ops, SparseCore 0:
  143.1 12.7 reduce-scatter.1
  157.6 13.2 all-gather.5
  172.5 13.2 all-gather.3
  187.3 13.2 all-gather.7
where the time goes:
time: 237 us; the launch traced here: 236 us
  blocking collectives  108 us (46%)
  waiting for transfers between devices  65.8 us (28%)
  local copies, waits for them, and re-layouts  17.2 us (7%)
  between operations  16 us (7%)
  matrix products  15 us (6%)
  other arithmetic  6.77 us (3%)
  starting transfers between devices  6.67 us (3%)
    all_to_all x1, blocking collectives, shards(): lax.all_to_all(outgoing_k, 'req', split_axis=0, concat_axis=0, tiled=True)  62.2 us
    all_to_all x1, waiting for transfers between devices, shards(): lax.all_to_all(outgoing_v, 'req', split_axis=0, concat_axis=0, tiled=True)  37.3 us
    all_to_all x1, blocking collectives, shards(): lax.all_to_all(result.reshape(senders, slot_count, feature_count), 'req',...  25 us
    all_to_all x1, blocking collectives, shards(): lax.all_to_all(outgoing, 'req', split_axis=0, concat_axis=0, tiled=True)  21 us
    all_gather x1, waiting for transfers between devices, shards(): lax.all_gather(w_down, 'kv', axis=2, tiled=True)  13 us
    reduce_scatter x1, waiting for transfers between devices, shards(): lax.psum_scatter(head_terms, 'kv', scatter_dimension=0, tiled=True)  9.87 us
    all_to_all x1, starting transfers between devices, shards(): lax.all_to_all(outgoing_v, 'req', split_axis=0, concat_axis=0, tiled=True)  6.51 us
  transfers between devices with their start and end apart: 5, of which 4 were waited for; matrix products, arithmetic and copies ran while one was open for 7% of the time, Pallas kernels for 0%

commit v1 on v0

v1 whole, which is shorter than its diff:
```python
import functools

import jax
import jax.numpy as jnp
from jax import lax
from jax.experimental import pallas as pl
from jax.experimental.pallas import tpu as pltpu
from jax.sharding import PartitionSpec as P

BF = jnp.bfloat16
F32 = jnp.float32
LAST = (((1,), (1,)), ((), ()))


def rms_scaled(wide, gain_row):
    squares = jnp.mean(wide * wide, axis=-1, keepdims=True)
    return (wide * lax.rsqrt(squares + 1e-06) * gain_row).astype(BF)


def wait_bytes(ref, sem):
    pltpu.make_async_copy(ref, ref, sem).wait()


def layer_kernel(
    n,
    pages_s,
    lengths_s,
    owner_s,
    routes_s,
    tokens_h,
    gains_h,
    wq_h,
    wk_h,
    wv_h,
    wo_h,
    ck_h,
    cv_h,
    wr_h,
    wg_h,
    wu_h,
    wd_h,
    out_ref,
    tok,
    gains,
    wqkv,
    wo,
    ck,
    cv,
    wr,
    wg,
    wu,
    wd,
    heads,
    scores,
    att,
    q_out,
    q_in,
    a_out,
    a_in,
    head_sum,
    head_in,
    wide_a,
    disp_out,
    disp_in,
    wide_b,
    ret_out,
    ret_in,
    load_sems,
    w_send,
    w_recv,
    h_send,
    h_recv,
    send_sems,
    recv_sems,
):
    me = lax.axis_index("req")
    kv = lax.axis_index("kv")
    slots, width = tok.shape
    half = slots // 2
    hd = ck.shape[2]
    page = ck.shape[1]
    per_slot = pages_s.shape[0]
    groups = wo.shape[0] // hd
    experts = n // 2
    cols = width // hd
    inv_root = hd ** (-0.5)

    def load(src, dst, i):
        copy = pltpu.make_async_copy(src, dst, load_sems.at[i])
        copy.start()
        return copy

    qcols = wq_h.shape[1]
    l_tok = load(tokens_h, tok, 0)
    l_gain = load(gains_h, gains, 1)
    l_wq = load(wq_h, wqkv.at[:, pl.ds(0, qcols)], 2)
    l_wk = load(wk_h, wqkv.at[:, pl.ds(qcols, hd)], 3)
    l_wv = load(wv_h, wqkv.at[:, pl.ds(qcols + hd, hd)], 4)
    l_ck = load(ck_h, ck, 5)
    l_cv = load(cv_h, cv, 6)
    l_wo = load(wo_h, wo, 7)
    l_wr = load(wr_h, wr, 8)
    l_wg = load(wg_h.at[0], wg.at[0], 9)
    l_wu = load(wu_h.at[0], wu.at[0], 10)
    l_wd = load(wd_h.at[0], wd.at[0], 11)

    barrier = pltpu.get_barrier_semaphore()

    def greet(i, carry):
        pl.semaphore_signal(barrier, 1, device_id={"req": lax.rem(me + i, n)})
        return carry

    pl.semaphore_signal(barrier, 1, device_id={"kv": 1 - kv})
    lax.fori_loop(1, n, greet, 0)

    def to_all(src_of, dst, phase):
        def send(i, carry):
            peer = lax.rem(me + i, n)
            pltpu.make_async_remote_copy(
                src_ref=src_of(peer),
                dst_ref=dst.at[me],
                send_sem=send_sems.at[phase],
                recv_sem=recv_sems.at[phase],
                device_id={"req": peer},
            ).start()
            return carry

        pltpu.make_async_copy(src_of(me), dst.at[me], recv_sems.at[phase]).start()
        lax.fori_loop(1, n, send, 0)

    l_tok.wait()
    l_gain.wait()
    tokf = tok[...].astype(F32)
    normed = rms_scaled(tokf, gains[0:1, :])
    l_wq.wait()
    l_wk.wait()
    l_wv.wait()
    qkv = jnp.dot(normed, wqkv[...], preferred_element_type=F32).astype(BF).astype(F32)
    for h in range(groups + 2):
        heads[pl.ds(h, slots, stride=8), :] = qkv[:, h * hd : (h + 1) * hd]
    last = (slots - 1) * 8
    q_out[...] = heads[last : last + 8, :].astype(BF)

    pl.semaphore_wait(barrier, n)
    to_all(lambda peer: q_out, q_in, 0)
    sibling = {"kv": 1 - kv}
    swaps = []
    for i, (src, dst) in enumerate(((wg_h, wg), (wu_h, wu), (wd_h, wd))):
        swap = pltpu.make_async_remote_copy(
            src_ref=src.at[0],
            dst_ref=dst.at[1],
            send_sem=w_send.at[i],
            recv_sem=w_recv.at[i],
            device_id=sibling,
        )
        swap.start()
        swaps.append(swap)

    def attend(first, count):
        rows = slice(first * 8, (first + count) * 8)
        place = lax.broadcasted_iota(jnp.int32, (8, page), 1)
        for s in range(first, first + count):
            block = heads[s * 8 : s * 8 + 8, :].astype(BF)
            live = lengths_s[me * slots + s]
            for j in range(per_slot):
                dots = lax.dot_general(
                    block, ck[pages_s[j, s]], LAST, preferred_element_type=F32
                )
                scores[s * 8 : s * 8 + 8, j * page : (j + 1) * page] = jnp.where(
                    place + j * page < live, dots * inv_root, -1e30
                )
        all_scores = scores[rows, :]
        top = jnp.max(all_scores, axis=-1, keepdims=True)
        weights = jnp.exp(all_scores - top)
        total = jnp.sum(weights, axis=-1, keepdims=True)
        scores[rows, :] = weights
        for s in range(first, first + count):
            acc = jnp.zeros((8, hd), F32)
            for j in range(per_slot):
                acc = acc + jnp.dot(
                    scores[s * 8 : s * 8 + 8, j * page : (j + 1) * page].astype(BF),
                    cv[pages_s[j, s]],
                    preferred_element_type=F32,
                )
            att[s * 8 : s * 8 + 8, :] = acc
        block = heads[rows, :].reshape(count, 8, hd)
        own = jnp.sum(block * block[:, groups : groups + 1, :], axis=-1, keepdims=True) * inv_root
        top = top.reshape(count, 8, 1)
        total = total.reshape(count, 8, 1)
        joint = jnp.maximum(top, own)
        old_part = jnp.exp(top - joint)
        new_part = jnp.exp(own - joint)
        merged = (
            att[rows, :].reshape(count, 8, hd) * old_part
            + new_part * block[:, groups + 1 : groups + 2, :]
        )
        result = merged / (total * old_part + new_part)
        att[rows, :] = result.astype(BF).astype(F32).reshape(count * 8, hd)

    l_ck.wait()
    l_cv.wait()
    attend(0, slots - 1)

    wait_bytes(q_in, recv_sems.at[0])
    heads[last : last + 8, :] = q_in[owner_s[me]].astype(F32)
    attend(slots - 1, 1)
    a_out[...] = att[last : last + 8, :].astype(BF)
    to_all(lambda peer: a_out, a_in, 1)

    def find(c, found):
        return jnp.where(owner_s[c] == me, c, found)

    origin = lax.fori_loop(0, n, find, 0)
    l_wo.wait()
    wait_bytes(a_in, recv_sems.at[1])
    att[last : last + 8, :] = a_in[origin].astype(F32)
    attended = jnp.concatenate(
        [att[pl.ds(h, slots, stride=8), :].astype(BF) for h in range(groups)], axis=1
    )
    terms = jnp.dot(attended, wo[...], preferred_element_type=F32)
    head_sum[0] = terms[:half]
    head_sum[1] = terms[half:]
    cross = pltpu.make_async_remote_copy(
        src_ref=head_sum.at[1 - kv],
        dst_ref=head_in,
        send_sem=h_send,
        recv_sem=h_recv,
        device_id=sibling,
    )
    cross.start()
    first_core = kv == 0
    mine = jnp.where(first_core, terms[:half], terms[half:])
    residual = jnp.where(first_core, tokf[:half], tokf[half:])
    cross.wait_recv()
    middle = (residual + (mine + head_in[...])).astype(BF).astype(F32)
    normed_two = rms_scaled(middle, gains[1:2, :])

    l_wr.wait()
    topk = routes_s.shape[0]
    lane = lax.broadcasted_iota(jnp.int32, (half, 128), 1)
    row = lax.broadcasted_iota(jnp.int32, (half, 128), 0)

    route = []
    for j in range(topk):
        named_by = jnp.zeros((half, 128), jnp.int32)
        for i in range(half):
            named_by = jnp.where(row == i, routes_s[j, i], named_by)
        route.append(named_by)

    def places(expert, slot):
        named = jnp.zeros((half, 128), F32)
        for j in range(topk):
            named = named + jnp.where(route[j] == expert, 1.0, 0.0)
        rank = jnp.zeros((half, 128), F32)
        for i in range(half - 1):
            rank = rank + jnp.where(row > i, named[i : i + 1, :], 0.0)
        return jnp.where(rank == slot.astype(F32), named, 0.0)

    pick = places(lane % experts, lane // experts)
    pick_t = jnp.transpose(pick)[: 2 * experts, :].astype(BF)
    outgoing = jnp.dot(pick_t, normed_two, preferred_element_type=F32)
    for c in range(cols):
        for k in range(2):
            wide_a[pl.ds(c * 2 + k, experts, stride=2 * cols), :] = outgoing[
                k * experts : (k + 1) * experts, c * hd : (c + 1) * hd
            ]
    disp_out[...] = wide_a[...].reshape(experts, 2 * cols, hd).astype(BF)
    to_all(lambda peer: disp_out.at[peer // 2], disp_in, 2)

    logits = lax.dot_general(normed_two, wr[...], LAST, preferred_element_type=F32)
    choice = lax.broadcasted_iota(jnp.int32, logits.shape, 1)
    chosen = [
        jnp.sum(jnp.where(choice == route[j][:, :experts], logits, 0.0), axis=-1, keepdims=True)
        for j in range(topk)
    ]
    best = functools.reduce(jnp.maximum, chosen)
    powers = [jnp.exp(c - best) for c in chosen]
    denom = functools.reduce(jnp.add, powers)
    peer_expert = (lane % n) // 2
    blend = jnp.zeros((half, 128), F32)
    for j in range(topk):
        blend = blend + jnp.where(route[j] == peer_expert, powers[j] / denom, 0.0)
    blend = blend * places(peer_expert, lane // n)
    part_a = blend.astype(BF).astype(F32)
    part_b = (blend - part_a).astype(BF).astype(F32)
    part_c = blend - part_a - part_b
    blend_parts = jnp.concatenate([part_a, part_b, part_c], axis=0).astype(BF)

    l_wg.wait()
    l_wu.wait()
    l_wd.wait()
    for swap in swaps:
        swap.wait_recv()
    wait_bytes(disp_in, recv_sems.at[2])
    wide_b[...] = disp_in[...].astype(F32).reshape(n * 2 * cols, hd)

    def unpack():
        return jnp.concatenate(
            [
                jnp.concatenate(
                    [
                        wide_b[pl.ds(c * 2 + k, n, stride=2 * cols), :].astype(BF)
                        for c in range(cols)
                    ],
                    axis=1,
                )
                for k in range(2)
            ],
            axis=0,
        )

    arrived = unpack()
    result = None
    for t in range(2):
        gate = lax.dot_general(arrived, wg[t], LAST, preferred_element_type=F32)
        up = lax.dot_general(arrived, wu[t], LAST, preferred_element_type=F32)
        hidden = (jnp.maximum(gate, 0.0) * up).astype(BF)
        part = jnp.dot(hidden, wd[t], preferred_element_type=F32)
        result = part if result is None else result + part
    for c in range(cols):
        for k in range(2):
            wide_b[pl.ds(c * 2 + k, n, stride=2 * cols), :] = result[
                k * n : (k + 1) * n, c * hd : (c + 1) * hd
            ]
    ret_out[...] = wide_b[...].reshape(n, 2 * cols, hd).astype(BF)
    to_all(lambda peer: ret_out.at[peer], ret_in, 3)
    wait_bytes(ret_in, recv_sems.at[3])
    wide_b[...] = ret_in[...].astype(F32).reshape(n * 2 * cols, hd)
    mixed = jnp.dot(blend_parts, unpack(), preferred_element_type=F32)
    mixed = mixed[:half] + mixed[half : 2 * half] + mixed[2 * half :]
    out_ref[...] = (middle + mixed).astype(BF)

    cross.wait_send()
    for swap in swaps:
        swap.wait_send()
    for phase, ref in enumerate((q_in, a_in, disp_in, ret_in)):
        wait_bytes(ref.at[pl.ds(0, n - 1)], send_sems.at[phase])


def solution(mesh):
    n = mesh.shape["req"]

    def shards(
        tokens,
        gain_attn,
        w_query,
        w_key,
        w_value,
        w_out,
        cache_k,
        cache_v,
        page_table,
        lengths,
        new_owner,
        gain_moe,
        w_router,
        routes,
        w_gate,
        w_up,
        w_down,
    ):
        slots, width = tokens.shape
        half = slots // 2
        hd = w_key.shape[1]
        cols = width // hd
        experts = n // 2
        span = page_table.shape[1] * cache_k.shape[1]
        gains = jnp.stack([gain_attn, gain_moe]).astype(F32)
        hidden = w_gate.shape[2]
        smem = pl.BlockSpec(memory_space=pltpu.SMEM)
        hbm = pl.BlockSpec(memory_space=pl.ANY)
        dma = pltpu.SemaphoreType.DMA
        return pl.pallas_call(
            functools.partial(layer_kernel, n),
            out_shape=jax.ShapeDtypeStruct((half, width), BF),
            in_specs=[smem] * 4 + [hbm] * 12,
            out_specs=pl.BlockSpec(memory_space=pltpu.VMEM),
            scratch_shapes=[
                pltpu.VMEM((slots, width), BF),
                pltpu.VMEM((2, width), F32),
                pltpu.VMEM((width, w_query.shape[1] + 2 * hd), BF),
                pltpu.VMEM(w_out.shape, BF),
                pltpu.VMEM(cache_k.shape, BF),
                pltpu.VMEM(cache_v.shape, BF),
                pltpu.VMEM(w_router.shape[::-1], BF),
                pltpu.VMEM((2, hidden, width), BF),
                pltpu.VMEM((2, hidden, width), BF),
                pltpu.VMEM((2, hidden, width), BF),
                pltpu.VMEM((slots * 8, hd), F32),
                pltpu.VMEM((slots * 8, span), F32),
                pltpu.VMEM((slots * 8, hd), F32),
                pltpu.VMEM((8, hd), BF),
                pltpu.VMEM((n, 8, hd), BF),
                pltpu.VMEM((8, hd), BF),
                pltpu.VMEM((n, 8, hd), BF),
                pltpu.VMEM((2, half, width), F32),
                pltpu.VMEM((half, width), F32),
                pltpu.VMEM((experts * 2 * cols, hd), F32),
                pltpu.VMEM((experts, 2 * cols, hd), BF),
                pltpu.VMEM((n, 2 * cols, hd), BF),
                pltpu.VMEM((n * 2 * cols, hd), F32),
                pltpu.VMEM((n, 2 * cols, hd), BF),
                pltpu.VMEM((n, 2 * cols, hd), BF),
                dma((12,)),
                dma((3,)),
                dma((3,)),
                dma,
                dma,
                dma((4,)),
                dma((4,)),
            ],
            compiler_params=pltpu.CompilerParams(
                collective_id=0, has_side_effects=True, vmem_limit_bytes=60 * 1024 * 1024
            ),
        )(
            page_table.T,
            lengths,
            new_owner,
            routes.T,
            tokens,
            gains,
            w_query,
            w_key,
            w_value,
            w_out,
            cache_k,
            cache_v,
            w_router.T,
            jnp.swapaxes(w_gate, 1, 2),
            jnp.swapaxes(w_up, 1, 2),
            jnp.swapaxes(w_down, 1, 2),
        )

    return jax.shard_map(
        shards,
        mesh=mesh,
        in_specs=(
            P("req", None),
            P(),
            P(None, "kv"),
            P(None, "kv"),
            P(None, "kv"),
            P("kv", None),
            P("req", None, "kv"),
            P("req", None, "kv"),
            P("req", None),
            P(),
            P(),
            P(),
            P(),
            P(("req", "kv"), None),
            P("req", None, "kv"),
            P("req", None, "kv"),
            P("req", None, "kv"),
        ),
        out_specs=P(("req", "kv"), None),
        check_vma=False,
    )
```

time: 237 us -> 47.6 us (0.20)
  blocking collectives: 108 us -> 0 us
  waiting for transfers between devices: 65.8 us -> 0 us
  Pallas kernels: 0 us -> 44 us
  between operations: 16 us -> 0.01 us
  matrix products: 15 us -> 0 us
  local copies, waits for them, and re-layouts: 17.2 us -> 2.73 us
  starting transfers between devices: 6.67 us -> 0 us
  other arithmetic: 6.77 us -> 0.62 us
    all_to_all x3 -> x0, blocking collectives: 108 us -> none  [the longest x1 62.2 us: shards(): lax.all_to_all(outgoing_k, 'req', split_axis=0, concat_axis=0, tiled=True)]
    pallas_call x0 -> x1, Pallas kernels: none -> 44 us  [shards(): pl.pallas_call(functools.partial(layer_kernel, n), out_shape=jax.ShapeDty...]
    all_to_all x1 -> x0, waiting for transfers between devices: 37.3 us -> none  [shards(): lax.all_to_all(outgoing_v, 'req', split_axis=0, concat_axis=0, tiled=True)]
    all_gather x3 -> x0, waiting for transfers between devices: 16.7 us -> none  [the longest x1 13 us: shards(): lax.all_gather(w_down, 'kv', axis=2, tiled=True)]
    dot_general x13 -> x0, matrix products: 15 us -> none  [the longest x1 2.31 us: cache_partial(): jnp.einsum('rgd,rtd->rgt', queries, page_keys, preferred_element_type=jnp...]
    reduce_scatter x1 -> x0, waiting for transfers between devices: 9.87 us -> none  [shards(): lax.psum_scatter(head_terms, 'kv', scatter_dimension=0, tiled=True)]
    gather x7 -> x0, local copies, waits for them, and re-layouts: 8.52 us -> none  [the longest x1 3.76 us: shards(): page_values = cache_v[page_table].reshape(req_dev, -1, head_dim)]
    all_to_all x1 -> x0, starting transfers between devices: 6.51 us -> none  [shards(): lax.all_to_all(outgoing_v, 'req', split_axis=0, concat_axis=0, tiled=True)]
  transfers between devices with their start and end apart: 5 -> 0, of which waited for: 4 -> 0; matrix products, arithmetic and copies ran while one was open for 7% -> 0% of each run, Pallas kernels for 0% -> 0%
where the time goes in v1:
time: 47.6 us; the launch traced here: 47.4 us
  Pallas kernels  44 us (92%)
  local copies, waits for them, and re-layouts  2.73 us (6%)
  other arithmetic  0.62 us (1%)
    pallas_call x1, Pallas kernels, shards(): pl.pallas_call(functools.partial(layer_kernel, n), out_shape=jax.ShapeDty...  44 us
    another operation x2, local copies, waits for them, and re-layouts, shards(): gains = jnp.stack([gain_attn, gain_moe]).astype(F32)  1.38 us
    unnamed x1, local copies, waits for them, and re-layouts  1.35 us

profile of v1, /device:TPU:1, one launch (start us, length us, event | category | flops | bytes accessed | tf_op | source)
XLA Modules:
  0.0 47.4 jit_solution(5678033012642937903)
XLA Ops:
  0.0 0.7 %stack.9 = bf16[1,1536]{1,0:T(2,128)(2,1)S(1)} reshape(bf16[1536]{0:T(1024)(128)(2,1)} %param.18) | data formatting | bytes 6144 | tf_op jit(solution)/shard_map/stack | solution.py:368
  0.7 0.7 %stack.10 = bf16[1,1536]{1,0:T(2,128)(2,1)S(1)} reshape(bf16[1536]{0:T(1024)(128)(2,1)} %param.28) | data formatting | bytes 6144 | tf_op jit(solution)/shard_map/stack | solution.py:368
  1.4 0.6 %maximum_convert_fusion.gains_h = f32[2,1536]{1,0:T(2,128)} fusion(bf16[1,1536]{1,0:T(2,128)(2,1)S(1)} %stack.10, bf16[1,1536]{1,0:T(2,128)(2,1)S(1)} %stack.9), kind=kLoop, calls=%fused_computation | loop fusion | flops 12288 | bytes 18432 | tf_op jit(solution)/shard_map/convert_element_type | solution.py:368
  2.0 44.0 %shard_map.163 = bf16[8,1536]{1,0:T(8,128)(2,1)} custom-call(s32[4,16]{1,0:T(4,128)} %bitcast.10, s32[1024]{0:T(1024)} %lengths_s.1, s32[64]{0:T(128)} %owner_s.1, s32[4,8]{1,0:T(4,128)} %bitcast.11, bf16[16,1536]{1,0:T(8,128)(2,1)} %tokens_h.1, f32[2,1536]{1,0:T(2,128)} %maximum_convert_fusion.gains_h, bf16[1536,768]{1,0:T(8,128)(2,1)} %wq_h.1, ...), custom_call_target="tpu_custom_call" | custom-call | tf_op jit(solution)/shard_map/pallas_call | solution.py:373
  46.0 1.3 %copy.19 = bf16[8,1536]{1,0:T(8,128)(2,1)} copy(bf16[8,1536]{1,0:T(8,128)(2,1)} %shard_map.163) | data formatting | bytes 49152

commit v2 on v1

--- a/solution.py
+++ b/solution.py
@@ -55,8 +55,6 @@
     att,
     q_out,
     q_in,
-    a_out,
-    a_in,
     head_sum,
     head_in,
     wide_a,
@@ -65,13 +63,28 @@
     wide_b,
     ret_out,
     ret_in,
+    fin,
+    row_sum,
+    row_in,
+    t_out,
+    t_in,
+    m_wide,
+    m_out,
+    m_in,
+    wide_m,
+    late_out,
+    late_in,
     load_sems,
     w_send,
     w_recv,
     h_send,
     h_recv,
+    r_send,
+    r_recv,
     send_sems,
     recv_sems,
+    line_x,
+    line_z,
 ):
     me = lax.axis_index("req")
     kv = lax.axis_index("kv")
@@ -104,14 +117,20 @@
     l_wu = load(wu_h.at[0], wu.at[0], 10)
     l_wd = load(wd_h.at[0], wd.at[0], 11)
 
+    def line(stride, i):
+        spot = lax.rem(me // stride, 4)
+        return {"req": me + (lax.rem(spot + i, 4) - spot) * stride}
+
+    def greet(sem, stride):
+        for i in range(1, 4):
+            pl.semaphore_signal(sem, 1, device_id=line(stride, i))
+
+    sibling = {"kv": 1 - kv}
+    relocating = kv == 1
     barrier = pltpu.get_barrier_semaphore()
-
-    def greet(i, carry):
-        pl.semaphore_signal(barrier, 1, device_id={"req": lax.rem(me + i, n)})
-        return carry
-
-    pl.semaphore_signal(barrier, 1, device_id={"kv": 1 - kv})
-    lax.fori_loop(1, n, greet, 0)
+    pl.semaphore_signal(barrier, 1, device_id=sibling)
+    for stride in (1, 4, 16):
+        greet(barrier, stride)
 
     def to_all(src_of, dst, phase):
         def send(i, carry):
@@ -132,18 +151,13 @@
     l_gain.wait()
     tokf = tok[...].astype(F32)
     normed = rms_scaled(tokf, gains[0:1, :])
-    l_wq.wait()
-    l_wk.wait()
-    l_wv.wait()
-    qkv = jnp.dot(normed, wqkv[...], preferred_element_type=F32).astype(BF).astype(F32)
-    for h in range(groups + 2):
-        heads[pl.ds(h, slots, stride=8), :] = qkv[:, h * hd : (h + 1) * hd]
     last = (slots - 1) * 8
-    q_out[...] = heads[last : last + 8, :].astype(BF)
-
-    pl.semaphore_wait(barrier, n)
-    to_all(lambda peer: q_out, q_in, 0)
-    sibling = {"kv": 1 - kv}
+    m_wide[...] = jnp.zeros((16, hd), F32)
+    for c in range(cols):
+        m_wide[c : c + 1, :] = tokf[slots - 1 : slots, c * hd : (c + 1) * hd]
+    t_out[...] = m_wide[...].astype(BF)
+    pl.semaphore_wait(barrier, 10)
+    greet(line_x, 4)
     swaps = []
     for i, (src, dst) in enumerate(((wg_h, wg), (wu_h, wu), (wd_h, wd))):
         swap = pltpu.make_async_remote_copy(
@@ -155,6 +169,21 @@
         )
         swap.start()
         swaps.append(swap)
+    pl.semaphore_wait(line_x, 3)
+    greet(line_z, 16)
+    l_wq.wait()
+    l_wk.wait()
+    l_wv.wait()
+    qkv = jnp.dot(normed, wqkv[...], preferred_element_type=F32).astype(BF).astype(F32)
+    for h in range(groups + 2):
+        heads[pl.ds(h, slots, stride=8), :] = qkv[:, h * hd : (h + 1) * hd]
+    q_out[...] = heads[last : last + 8, :].astype(BF)
+    pl.semaphore_wait(line_z, 3)
+    to_all(lambda peer: q_out, q_in, 0)
+
+    @pl.when(relocating)
+    def _():
+        to_all(lambda peer: t_out, t_in, 1)
 
     def attend(first, count):
         rows = slice(first * 8, (first + count) * 8)
@@ -200,24 +229,16 @@
     l_ck.wait()
     l_cv.wait()
     attend(0, slots - 1)
-
-    wait_bytes(q_in, recv_sems.at[0])
-    heads[last : last + 8, :] = q_in[owner_s[me]].astype(F32)
-    attend(slots - 1, 1)
-    a_out[...] = att[last : last + 8, :].astype(BF)
-    to_all(lambda peer: a_out, a_in, 1)
-
-    def find(c, found):
-        return jnp.where(owner_s[c] == me, c, found)
-
-    origin = lax.fori_loop(0, n, find, 0)
+    att[last : last + 8, :] = jnp.zeros((8, hd), F32)
     l_wo.wait()
-    wait_bytes(a_in, recv_sems.at[1])
-    att[last : last + 8, :] = a_in[origin].astype(F32)
-    attended = jnp.concatenate(
-        [att[pl.ds(h, slots, stride=8), :].astype(BF) for h in range(groups)], axis=1
-    )
-    terms = jnp.dot(attended, wo[...], preferred_element_type=F32)
+
+    def head_terms():
+        attended = jnp.concatenate(
+            [att[pl.ds(h, slots, stride=8), :].astype(BF) for h in range(groups)], axis=1
+        )
+        return jnp.dot(attended, wo[...], preferred_element_type=F32)
+
+    terms = head_terms()
     head_sum[0] = terms[:half]
     head_sum[1] = terms[half:]
     cross = pltpu.make_async_remote_copy(
@@ -231,26 +252,23 @@
     first_core = kv == 0
     mine = jnp.where(first_core, terms[:half], terms[half:])
     residual = jnp.where(first_core, tokf[:half], tokf[half:])
-    cross.wait_recv()
-    middle = (residual + (mine + head_in[...])).astype(BF).astype(F32)
-    normed_two = rms_scaled(middle, gains[1:2, :])
-
-    l_wr.wait()
+
     topk = routes_s.shape[0]
     lane = lax.broadcasted_iota(jnp.int32, (half, 128), 1)
     row = lax.broadcasted_iota(jnp.int32, (half, 128), 0)
-
+    late_row = (row == half - 1) & relocating
     route = []
     for j in range(topk):
         named_by = jnp.zeros((half, 128), jnp.int32)
         for i in range(half):
             named_by = jnp.where(row == i, routes_s[j, i], named_by)
         route.append(named_by)
+    early = [jnp.where(late_row, -1, r) for r in route]
 
     def places(expert, slot):
         named = jnp.zeros((half, 128), F32)
         for j in range(topk):
-            named = named + jnp.where(route[j] == expert, 1.0, 0.0)
+            named = named + jnp.where(early[j] == expert, 1.0, 0.0)
         rank = jnp.zeros((half, 128), F32)
         for i in range(half - 1):
             rank = rank + jnp.where(row > i, named[i : i + 1, :], 0.0)
@@ -258,6 +276,12 @@
 
     pick = places(lane % experts, lane // experts)
     pick_t = jnp.transpose(pick)[: 2 * experts, :].astype(BF)
+    peer_expert = (lane % n) // 2
+    peer_place = places(peer_expert, lane // n)
+
+    cross.wait_recv()
+    middle = (residual + (mine + head_in[...])).astype(BF).astype(F32)
+    normed_two = rms_scaled(middle, gains[1:2, :])
     outgoing = jnp.dot(pick_t, normed_two, preferred_element_type=F32)
     for c in range(cols):
         for k in range(2):
@@ -267,24 +291,84 @@
     disp_out[...] = wide_a[...].reshape(experts, 2 * cols, hd).astype(BF)
     to_all(lambda peer: disp_out.at[peer // 2], disp_in, 2)
 
-    logits = lax.dot_general(normed_two, wr[...], LAST, preferred_element_type=F32)
-    choice = lax.broadcasted_iota(jnp.int32, logits.shape, 1)
-    chosen = [
-        jnp.sum(jnp.where(choice == route[j][:, :experts], logits, 0.0), axis=-1, keepdims=True)
-        for j in range(topk)
-    ]
-    best = functools.reduce(jnp.maximum, chosen)
-    powers = [jnp.exp(c - best) for c in chosen]
-    denom = functools.reduce(jnp.add, powers)
-    peer_expert = (lane % n) // 2
-    blend = jnp.zeros((half, 128), F32)
-    for j in range(topk):
-        blend = blend + jnp.where(route[j] == peer_expert, powers[j] / denom, 0.0)
-    blend = blend * places(peer_expert, lane // n)
-    part_a = blend.astype(BF).astype(F32)
-    part_b = (blend - part_a).astype(BF).astype(F32)
-    part_c = blend - part_a - part_b
-    blend_parts = jnp.concatenate([part_a, part_b, part_c], axis=0).astype(BF)
+    wait_bytes(q_in, recv_sems.at[0])
+    served = owner_s[me]
+    heads[last : last + 8, :] = q_in[served].astype(F32)
+    attend(slots - 1, 1)
+    late_terms = head_terms()[slots - 1 : slots, :]
+    row_sum[...] = late_terms
+
+    def row_copy():
+        return pltpu.make_async_remote_copy(
+            src_ref=row_sum,
+            dst_ref=row_in,
+            send_sem=r_send,
+            recv_sem=r_recv,
+            device_id=sibling,
+        )
+
+    @pl.when(first_core)
+    def _():
+        row_copy().start()
+
+    l_wr.wait()
+
+    def route_weights(normed_rows, chosen_by):
+        logits = lax.dot_general(normed_rows, wr[...], LAST, preferred_element_type=F32)
+        choice = lax.broadcasted_iota(jnp.int32, logits.shape, 1)
+        chosen = [
+            jnp.sum(jnp.where(choice == r[:, :experts], logits, 0.0), axis=-1, keepdims=True)
+            for r in chosen_by
+        ]
+        best = functools.reduce(jnp.maximum, chosen)
+        powers = [jnp.exp(c - best) for c in chosen]
+        denom = functools.reduce(jnp.add, powers)
+        blend = jnp.zeros((half, 128), F32)
+        for r, power in zip(chosen_by, powers):
+            blend = blend + jnp.where(r == peer_expert, power / denom, 0.0)
+        return blend
+
+    def in_parts(blend):
+        part_a = blend.astype(BF).astype(F32)
+        part_b = (blend - part_a).astype(BF).astype(F32)
+        part_c = blend - part_a - part_b
+        return jnp.concatenate([part_a, part_b, part_c], axis=0).astype(BF)
+
+    def blended(parts, rows):
+        mixed = jnp.dot(parts, rows, preferred_element_type=F32)
+        return mixed[:half] + mixed[half : 2 * half] + mixed[2 * half :]
+
+    blend_parts = in_parts(route_weights(normed_two, early) * peer_place)
+
+    @pl.when(relocating)
+    def _():
+        wait_bytes(t_in, recv_sems.at[1])
+        row_copy().wait_recv()
+        total = row_sum[...] + row_in[...]
+        for c in range(cols):
+            m_wide[c : c + 1, :] = total[:, c * hd : (c + 1) * hd]
+        m_out[...] = (t_in[served].astype(F32) + m_wide[...]).astype(BF)
+        to_all(lambda peer: m_out, m_in, 3)
+
+    def run_expert(rows):
+        result = None
+        for t in range(2):
+            gate = lax.dot_general(rows, wg[t], LAST, preferred_element_type=F32)
+            up = lax.dot_general(rows, wu[t], LAST, preferred_element_type=F32)
+            hidden = (jnp.maximum(gate, 0.0) * up).astype(BF)
+            part = jnp.dot(hidden, wd[t], preferred_element_type=F32)
+            result = part if result is None else result + part
+        return result
+
+    def unpack(wide, first, stride):
+        return jnp.concatenate(
+            [wide[pl.ds(first(c), n, stride=stride), :] for c in range(cols)], axis=1
+        )
+
+    def unpack_pair():
+        return jnp.concatenate(
+            [unpack(wide_b, lambda c: c * 2 + k, 2 * cols).astype(BF) for k in range(2)], axis=0
+        )
 
     l_wg.wait()
     l_wu.wait()
@@ -293,48 +377,73 @@
         swap.wait_recv()
     wait_bytes(disp_in, recv_sems.at[2])
     wide_b[...] = disp_in[...].astype(F32).reshape(n * 2 * cols, hd)
-
-    def unpack():
-        return jnp.concatenate(
-            [
-                jnp.concatenate(
-                    [
-                        wide_b[pl.ds(c * 2 + k, n, stride=2 * cols), :].astype(BF)
-                        for c in range(cols)
-                    ],
-                    axis=1,
-                )
-                for k in range(2)
-            ],
-            axis=0,
-        )
-
-    arrived = unpack()
-    result = None
-    for t in range(2):
-        gate = lax.dot_general(arrived, wg[t], LAST, preferred_element_type=F32)
-        up = lax.dot_general(arrived, wu[t], LAST, preferred_element_type=F32)
-        hidden = (jnp.maximum(gate, 0.0) * up).astype(BF)
-        part = jnp.dot(hidden, wd[t], preferred_element_type=F32)
-        result = part if result is None else result + part
+    result = run_expert(unpack_pair())
     for c in range(cols):
         for k in range(2):
             wide_b[pl.ds(c * 2 + k, n, stride=2 * cols), :] = result[
                 k * n : (k + 1) * n, c * hd : (c + 1) * hd
             ]
     ret_out[...] = wide_b[...].reshape(n, 2 * cols, hd).astype(BF)
-    to_all(lambda peer: ret_out.at[peer], ret_in, 3)
-    wait_bytes(ret_in, recv_sems.at[3])
+    to_all(lambda peer: ret_out.at[peer], ret_in, 4)
+
+    @pl.when(relocating)
+    def _():
+        owners = jnp.zeros((8, 128), jnp.int32)
+        owner_lane = lax.broadcasted_iota(jnp.int32, (8, 128), 1)
+        for c in range(n):
+            owners = jnp.where(owner_lane == c, owner_s[c], owners)
+        slot_row = lax.broadcasted_iota(jnp.int32, (n, n), 0)
+        moves = jnp.where(slot_row == owners[0:1, :n], 1.0, 0.0).astype(BF)
+        wait_bytes(m_in, recv_sems.at[3])
+        wide_m[...] = m_in[...].astype(F32).reshape(n * 16, hd)
+        late_normed = rms_scaled(unpack(wide_m, lambda c: c, 16), gains[1:2, :])
+        ordered = jnp.dot(moves, late_normed, preferred_element_type=F32).astype(BF)
+        late_result = run_expert(ordered)
+
+        def find(c, found):
+            return jnp.where(owner_s[c] == me, c, found)
+
+        origin = lax.fori_loop(0, n, find, 0)
+        late_middle = jnp.concatenate(
+            [wide_m[pl.ds(origin * 16 + c, 1), :] for c in range(cols)], axis=1
+        )
+        late_middle = jnp.broadcast_to(late_middle, (half, width))
+        late_blend = in_parts(
+            jnp.where(
+                lane < n,
+                route_weights(rms_scaled(late_middle, gains[1:2, :]), route),
+                0.0,
+            )[:, :n]
+        )
+        for c in range(cols):
+            wide_m[pl.ds(c, n, stride=16), :] = late_result[:, c * hd : (c + 1) * hd]
+        late_out[...] = wide_m[...].reshape(n, 16, hd).astype(BF)
+        to_all(lambda peer: late_out.at[peer], late_in, 5)
+        wait_bytes(late_in, recv_sems.at[5])
+        wide_m[...] = late_in[...].astype(F32).reshape(n * 16, hd)
+        late = late_middle + blended(late_blend, unpack(wide_m, lambda c: c, 16).astype(BF))
+        fin[half - 1 : half, :] = late[half - 1 : half, :]
+
+    wait_bytes(ret_in, recv_sems.at[4])
     wide_b[...] = ret_in[...].astype(F32).reshape(n * 2 * cols, hd)
-    mixed = jnp.dot(blend_parts, unpack(), preferred_element_type=F32)
-    mixed = mixed[:half] + mixed[half : 2 * half] + mixed[2 * half :]
-    out_ref[...] = (middle + mixed).astype(BF)
+    done = middle + blended(blend_parts, unpack_pair())
+    kept = (lax.broadcasted_iota(jnp.int32, (half, width), 0) == half - 1) & relocating
+    out_ref[...] = jnp.where(kept, fin[...], done).astype(BF)
 
     cross.wait_send()
     for swap in swaps:
         swap.wait_send()
-    for phase, ref in enumerate((q_in, a_in, disp_in, ret_in)):
+    for phase, ref in ((0, q_in), (2, disp_in), (4, ret_in)):
         wait_bytes(ref.at[pl.ds(0, n - 1)], send_sems.at[phase])
+
+    @pl.when(first_core)
+    def _():
+        row_copy().wait_send()
+
+    @pl.when(relocating)
+    def _():
+        for phase, ref in ((1, t_in), (3, m_in), (5, late_in)):
+            wait_bytes(ref.at[pl.ds(0, n - 1)], send_sems.at[phase])
 
 
 def solution(mesh):
@@ -391,8 +500,6 @@
                 pltpu.VMEM((slots * 8, hd), F32),
                 pltpu.VMEM((8, hd), BF),
                 pltpu.VMEM((n, 8, hd), BF),
-                pltpu.VMEM((8, hd), BF),
-                pltpu.VMEM((n, 8, hd), BF),
                 pltpu.VMEM((2, half, width), F32),
                 pltpu.VMEM((half, width), F32),
                 pltpu.VMEM((experts * 2 * cols, hd), F32),
@@ -401,13 +508,28 @@
                 pltpu.VMEM((n * 2 * cols, hd), F32),
                 pltpu.VMEM((n, 2 * cols, hd), BF),
                 pltpu.VMEM((n, 2 * cols, hd), BF),
+                pltpu.VMEM((half, width), F32),
+                pltpu.VMEM((1, width), F32),
+                pltpu.VMEM((1, width), F32),
+                pltpu.VMEM((16, hd), BF),
+                pltpu.VMEM((n, 16, hd), BF),
+                pltpu.VMEM((16, hd), F32),
+                pltpu.VMEM((16, hd), BF),
+                pltpu.VMEM((n, 16, hd), BF),
+                pltpu.VMEM((n * 16, hd), F32),
+                pltpu.VMEM((n, 16, hd), BF),
+                pltpu.VMEM((n, 16, hd), BF),
                 dma((12,)),
                 dma((3,)),
                 dma((3,)),
                 dma,
                 dma,
-                dma((4,)),
-                dma((4,)),
+                dma,
+                dma,
+                dma((6,)),
+                dma((6,)),
+                pltpu.SemaphoreType.REGULAR,
+                pltpu.SemaphoreType.REGULAR,
             ],
             compiler_params=pltpu.CompilerParams(
                 collective_id=0, has_side_effects=True, vmem_limit_bytes=60 * 1024 * 1024

time: 47.6 us -> 41 us (0.86)
  Pallas kernels: 44 us -> 37.4 us
    pallas_call x1, Pallas kernels: 44 us -> 37.4 us  [shards(): pl.pallas_call(functools.partial(layer_kernel, n), out_shape=jax.ShapeDty...]
where the time goes in v2:
time: 41 us; the launch traced here: 40.7 us
  Pallas kernels  37.4 us (91%)
  local copies, waits for them, and re-layouts  2.73 us (7%)
  other arithmetic  0.62 us (2%)
    pallas_call x1, Pallas kernels, shards(): pl.pallas_call(functools.partial(layer_kernel, n), out_shape=jax.ShapeDty...  37.4 us
    another operation x2, local copies, waits for them, and re-layouts, shards(): gains = jnp.stack([gain_attn, gain_moe]).astype(F32)  1.38 us
    unnamed x1, local copies, waits for them, and re-layouts  1.35 us

profile of v2, /device:TPU:1, one launch (start us, length us, event | category | flops | bytes accessed | tf_op | source)
XLA Modules:
  0.0 40.7 jit_solution(12374477601286928421)
XLA Ops:
  0.0 0.7 %stack.9 = bf16[1,1536]{1,0:T(2,128)(2,1)S(1)} reshape(bf16[1536]{0:T(1024)(128)(2,1)} %param.18) | data formatting | bytes 6144 | tf_op jit(solution)/shard_map/stack | solution.py:477
  0.7 0.7 %stack.10 = bf16[1,1536]{1,0:T(2,128)(2,1)S(1)} reshape(bf16[1536]{0:T(1024)(128)(2,1)} %param.28) | data formatting | bytes 6144 | tf_op jit(solution)/shard_map/stack | solution.py:477
  1.4 0.6 %maximum_convert_fusion.gains_h = f32[2,1536]{1,0:T(2,128)} fusion(bf16[1,1536]{1,0:T(2,128)(2,1)S(1)} %stack.10, bf16[1,1536]{1,0:T(2,128)(2,1)S(1)} %stack.9), kind=kLoop, calls=%fused_computation | loop fusion | flops 12288 | bytes 18432 | tf_op jit(solution)/shard_map/convert_element_type | solution.py:477
  2.0 37.4 %shard_map.163 = bf16[8,1536]{1,0:T(8,128)(2,1)} custom-call(s32[4,16]{1,0:T(4,128)} %bitcast.10, s32[1024]{0:T(1024)} %lengths_s.1, s32[64]{0:T(128)} %owner_s.1, s32[4,8]{1,0:T(4,128)} %bitcast.11, bf16[16,1536]{1,0:T(8,128)(2,1)} %tokens_h.1, f32[2,1536]{1,0:T(2,128)} %maximum_convert_fusion.gains_h, bf16[1536,768]{1,0:T(8,128)(2,1)} %wq_h.1, ...), custom_call_target="tpu_custom_call" | custom-call | tf_op jit(solution)/shard_map/pallas_call | solution.py:482
  39.4 1.3 %copy.19 = bf16[8,1536]{1,0:T(8,128)(2,1)} copy(bf16[8,1536]{1,0:T(8,128)(2,1)} %shard_map.163) | data formatting | bytes 49152

commit v3 on v2

--- a/solution.py
+++ b/solution.py
@@ -23,12 +23,13 @@
 
 def layer_kernel(
     n,
-    pages_s,
-    lengths_s,
-    owner_s,
-    routes_s,
+    pages_h,
+    lengths_h,
+    owner_h,
+    routes_h,
     tokens_h,
-    gains_h,
+    gain_a_h,
+    gain_m_h,
     wq_h,
     wk_h,
     wv_h,
@@ -41,7 +42,8 @@
     wd_h,
     out_ref,
     tok,
-    gains,
+    gain_a,
+    gain_m,
     wqkv,
     wo,
     ck,
@@ -63,6 +65,10 @@
     wide_b,
     ret_out,
     ret_in,
+    pages_s,
+    lengths_s,
+    owner_s,
+    routes_s,
     fin,
     row_sum,
     row_in,
@@ -83,8 +89,6 @@
     r_recv,
     send_sems,
     recv_sems,
-    line_x,
-    line_z,
 ):
     me = lax.axis_index("req")
     kv = lax.axis_index("kv")
@@ -105,10 +109,33 @@
 
     qcols = wq_h.shape[1]
     l_tok = load(tokens_h, tok, 0)
-    l_gain = load(gains_h, gains, 1)
+    l_gain = load(gain_a_h, gain_a, 1)
+    l_gain_m = load(gain_m_h, gain_m, 12)
     l_wq = load(wq_h, wqkv.at[:, pl.ds(0, qcols)], 2)
     l_wk = load(wk_h, wqkv.at[:, pl.ds(qcols, hd)], 3)
     l_wv = load(wv_h, wqkv.at[:, pl.ds(qcols + hd, hd)], 4)
+
+    sibling = {"kv": 1 - kv}
+    relocating = kv == 1
+    barrier = pltpu.get_barrier_semaphore()
+
+    def greet(i, carry):
+        pl.semaphore_signal(barrier, 1, device_id={"req": lax.rem(me + i, n)})
+        return carry
+
+    pl.semaphore_signal(barrier, 1, device_id=sibling)
+    lax.fori_loop(1, n, greet, 0)
+    l_ints = [
+        load(src, dst, 13 + i)
+        for i, (src, dst) in enumerate(
+            (
+                (pages_h, pages_s),
+                (lengths_h, lengths_s),
+                (owner_h, owner_s),
+                (routes_h, routes_s),
+            )
+        )
+    ]
     l_ck = load(ck_h, ck, 5)
     l_cv = load(cv_h, cv, 6)
     l_wo = load(wo_h, wo, 7)
@@ -116,21 +143,6 @@
     l_wg = load(wg_h.at[0], wg.at[0], 9)
     l_wu = load(wu_h.at[0], wu.at[0], 10)
     l_wd = load(wd_h.at[0], wd.at[0], 11)
-
-    def line(stride, i):
-        spot = lax.rem(me // stride, 4)
-        return {"req": me + (lax.rem(spot + i, 4) - spot) * stride}
-
-    def greet(sem, stride):
-        for i in range(1, 4):
-            pl.semaphore_signal(sem, 1, device_id=line(stride, i))
-
-    sibling = {"kv": 1 - kv}
-    relocating = kv == 1
-    barrier = pltpu.get_barrier_semaphore()
-    pl.semaphore_signal(barrier, 1, device_id=sibling)
-    for stride in (1, 4, 16):
-        greet(barrier, stride)
 
     def to_all(src_of, dst, phase):
         def send(i, carry):
@@ -149,15 +161,30 @@
 
     l_tok.wait()
     l_gain.wait()
+    l_gain_m.wait()
+    gain_attn = gain_a[...].astype(F32).reshape(1, width)
+    gain_moe = gain_m[...].astype(F32).reshape(1, width)
     tokf = tok[...].astype(F32)
-    normed = rms_scaled(tokf, gains[0:1, :])
+    normed = rms_scaled(tokf, gain_attn)
     last = (slots - 1) * 8
     m_wide[...] = jnp.zeros((16, hd), F32)
     for c in range(cols):
         m_wide[c : c + 1, :] = tokf[slots - 1 : slots, c * hd : (c + 1) * hd]
     t_out[...] = m_wide[...].astype(BF)
-    pl.semaphore_wait(barrier, 10)
-    greet(line_x, 4)
+    l_wq.wait()
+    l_wk.wait()
+    l_wv.wait()
+    qkv = jnp.dot(normed, wqkv[...], preferred_element_type=F32).astype(BF).astype(F32)
+    for h in range(groups + 2):
+        heads[pl.ds(h, slots, stride=8), :] = qkv[:, h * hd : (h + 1) * hd]
+    q_out[...] = heads[last : last + 8, :].astype(BF)
+    pl.semaphore_wait(barrier, n)
+    to_all(lambda peer: q_out, q_in, 0)
+
+    @pl.when(relocating)
+    def _():
+        to_all(lambda peer: t_out, t_in, 1)
+
     swaps = []
     for i, (src, dst) in enumerate(((wg_h, wg), (wu_h, wu), (wd_h, wd))):
         swap = pltpu.make_async_remote_copy(
@@ -169,21 +196,6 @@
         )
         swap.start()
         swaps.append(swap)
-    pl.semaphore_wait(line_x, 3)
-    greet(line_z, 16)
-    l_wq.wait()
-    l_wk.wait()
-    l_wv.wait()
-    qkv = jnp.dot(normed, wqkv[...], preferred_element_type=F32).astype(BF).astype(F32)
-    for h in range(groups + 2):
-        heads[pl.ds(h, slots, stride=8), :] = qkv[:, h * hd : (h + 1) * hd]
-    q_out[...] = heads[last : last + 8, :].astype(BF)
-    pl.semaphore_wait(line_z, 3)
-    to_all(lambda peer: q_out, q_in, 0)
-
-    @pl.when(relocating)
-    def _():
-        to_all(lambda peer: t_out, t_in, 1)
 
     def attend(first, count):
         rows = slice(first * 8, (first + count) * 8)
@@ -226,6 +238,8 @@
         result = merged / (total * old_part + new_part)
         att[rows, :] = result.astype(BF).astype(F32).reshape(count * 8, hd)
 
+    for l_int in l_ints:
+        l_int.wait()
     l_ck.wait()
     l_cv.wait()
     attend(0, slots - 1)
@@ -281,7 +295,7 @@
 
     cross.wait_recv()
     middle = (residual + (mine + head_in[...])).astype(BF).astype(F32)
-    normed_two = rms_scaled(middle, gains[1:2, :])
+    normed_two = rms_scaled(middle, gain_moe)
     outgoing = jnp.dot(pick_t, normed_two, preferred_element_type=F32)
     for c in range(cols):
         for k in range(2):
@@ -396,7 +410,7 @@
         moves = jnp.where(slot_row == owners[0:1, :n], 1.0, 0.0).astype(BF)
         wait_bytes(m_in, recv_sems.at[3])
         wide_m[...] = m_in[...].astype(F32).reshape(n * 16, hd)
-        late_normed = rms_scaled(unpack(wide_m, lambda c: c, 16), gains[1:2, :])
+        late_normed = rms_scaled(unpack(wide_m, lambda c: c, 16), gain_moe)
         ordered = jnp.dot(moves, late_normed, preferred_element_type=F32).astype(BF)
         late_result = run_expert(ordered)
 
@@ -411,7 +425,7 @@
         late_blend = in_parts(
             jnp.where(
                 lane < n,
-                route_weights(rms_scaled(late_middle, gains[1:2, :]), route),
+                route_weights(rms_scaled(late_middle, gain_moe), route),
                 0.0,
             )[:, :n]
         )
@@ -474,19 +488,18 @@
         cols = width // hd
         experts = n // 2
         span = page_table.shape[1] * cache_k.shape[1]
-        gains = jnp.stack([gain_attn, gain_moe]).astype(F32)
         hidden = w_gate.shape[2]
-        smem = pl.BlockSpec(memory_space=pltpu.SMEM)
         hbm = pl.BlockSpec(memory_space=pl.ANY)
         dma = pltpu.SemaphoreType.DMA
         return pl.pallas_call(
             functools.partial(layer_kernel, n),
             out_shape=jax.ShapeDtypeStruct((half, width), BF),
-            in_specs=[smem] * 4 + [hbm] * 12,
+            in_specs=[hbm] * 4 + [hbm] * 13,
             out_specs=pl.BlockSpec(memory_space=pltpu.VMEM),
             scratch_shapes=[
                 pltpu.VMEM((slots, width), BF),
-                pltpu.VMEM((2, width), F32),
+                pltpu.VMEM((width,), BF),
+                pltpu.VMEM((width,), BF),
                 pltpu.VMEM((width, w_query.shape[1] + 2 * hd), BF),
                 pltpu.VMEM(w_out.shape, BF),
                 pltpu.VMEM(cache_k.shape, BF),
@@ -508,6 +521,10 @@
                 pltpu.VMEM((n * 2 * cols, hd), F32),
                 pltpu.VMEM((n, 2 * cols, hd), BF),
                 pltpu.VMEM((n, 2 * cols, hd), BF),
+                pltpu.SMEM(page_table.shape[::-1], jnp.int32),
+                pltpu.SMEM(lengths.shape, jnp.int32),
+                pltpu.SMEM(new_owner.shape, jnp.int32),
+                pltpu.SMEM(routes.shape[::-1], jnp.int32),
                 pltpu.VMEM((half, width), F32),
                 pltpu.VMEM((1, width), F32),
                 pltpu.VMEM((1, width), F32),
@@ -519,7 +536,7 @@
                 pltpu.VMEM((n * 16, hd), F32),
                 pltpu.VMEM((n, 16, hd), BF),
                 pltpu.VMEM((n, 16, hd), BF),
-                dma((12,)),
+                dma((17,)),
                 dma((3,)),
                 dma((3,)),
                 dma,
@@ -528,8 +545,6 @@
                 dma,
                 dma((6,)),
                 dma((6,)),
-                pltpu.SemaphoreType.REGULAR,
-                pltpu.SemaphoreType.REGULAR,
             ],
             compiler_params=pltpu.CompilerParams(
                 collective_id=0, has_side_effects=True, vmem_limit_bytes=60 * 1024 * 1024
@@ -540,7 +555,8 @@
             new_owner,
             routes.T,
             tokens,
-            gains,
+            gain_attn,
+            gain_moe,
             w_query,
             w_key,
             w_value,

time: 41 us -> 36.9 us (0.90)
  Pallas kernels: 37.4 us -> 35.4 us
  local copies, waits for them, and re-layouts: 2.73 us -> 1.35 us
  other arithmetic: 0.62 us -> 0 us
    pallas_call x1, Pallas kernels: 37.4 us -> 35.4 us  [shards(): pl.pallas_call(functools.partial(layer_kernel, n), out_shape=jax.ShapeDty...]
    another operation x2 -> x0, local copies, waits for them, and re-layouts: 1.38 us -> none  [shards(): gains = jnp.stack([gain_attn, gain_moe]).astype(F32)]
    convert_element_type x1 -> x0, other arithmetic: 0.62 us -> none  [shards(): gains = jnp.stack([gain_attn, gain_moe]).astype(F32)]
where the time goes in v3:
time: 36.9 us; the launch traced here: 36.8 us
  Pallas kernels  35.4 us (96%)
  local copies, waits for them, and re-layouts  1.35 us (4%)
    pallas_call x1, Pallas kernels, shards(): pl.pallas_call(functools.partial(layer_kernel, n), out_shape=jax.ShapeDty...  35.4 us
    unnamed x1, local copies, waits for them, and re-layouts  1.35 us

profile of v3, /device:TPU:1, one launch (start us, length us, event | category | flops | bytes accessed | tf_op | source)
XLA Modules:
  0.0 36.8 jit_solution(3969395609595916350)
XLA Ops:
  0.0 35.4 %shard_map.163 = bf16[8,1536]{1,0:T(8,128)(2,1)} custom-call(s32[4,16]{1,0:T(4,128)} %bitcast.10, s32[1024]{0:T(1024)} %lengths_h.1, s32[64]{0:T(128)} %owner_h.1, s32[4,8]{1,0:T(4,128)} %bitcast.11, bf16[16,1536]{1,0:T(8,128)(2,1)} %tokens_h.1, bf16[1536]{0:T(1024)(128)(2,1)} %gain_a_h.1, bf16[1536]{0:T(1024)(128)(2,1)} %gain_m_h.1, ...), custom_call_target="tpu_custom_call" | custom-call | tf_op jit(solution)/shard_map/pallas_call | solution.py:494
  35.4 1.3 %copy.19 = bf16[8,1536]{1,0:T(8,128)(2,1)} copy(bf16[8,1536]{1,0:T(8,128)(2,1)} %shard_map.163) | data formatting | bytes 49152

commit v4 on v3

--- a/solution.py
+++ b/solution.py
@@ -1,4 +1,5 @@
 import functools
+import itertools
 
 import jax
 import jax.numpy as jnp
@@ -144,9 +145,22 @@
     l_wu = load(wu_h.at[0], wu.at[0], 10)
     l_wd = load(wd_h.at[0], wd.at[0], 11)
 
+    side = round(n ** (1 / 3))
+    me_z, me_x, me_y = me // (side * side), lax.rem(me // side, side), lax.rem(me, side)
+    at_z = [lax.rem(me_z + d, side) * (side * side) for d in range(side)]
+    at_x = [lax.rem(me_x + d, side) * side for d in range(side)]
+    at_y = [lax.rem(me_y + d, side) for d in range(side)]
+
+    def hops(offset):
+        return sum(min(d, side - d) for d in offset)
+
+    offsets = sorted(
+        (o for o in itertools.product(range(side), repeat=3) if any(o)), key=lambda o: -hops(o)
+    )
+
     def to_all(src_of, dst, phase):
-        def send(i, carry):
-            peer = lax.rem(me + i, n)
+        for dz, dx, dy in offsets:
+            peer = at_z[dz] + at_x[dx] + at_y[dy]
             pltpu.make_async_remote_copy(
                 src_ref=src_of(peer),
                 dst_ref=dst.at[me],
@@ -154,10 +168,7 @@
                 recv_sem=recv_sems.at[phase],
                 device_id={"req": peer},
             ).start()
-            return carry
-
         pltpu.make_async_copy(src_of(me), dst.at[me], recv_sems.at[phase]).start()
-        lax.fori_loop(1, n, send, 0)
 
     l_tok.wait()
     l_gain.wait()
@@ -493,7 +504,7 @@
         dma = pltpu.SemaphoreType.DMA
         return pl.pallas_call(
             functools.partial(layer_kernel, n),
-            out_shape=jax.ShapeDtypeStruct((half, width), BF),
+            out_shape=pltpu.VMEM((half, width), BF),
             in_specs=[hbm] * 4 + [hbm] * 13,
             out_specs=pl.BlockSpec(memory_space=pltpu.VMEM),
             scratch_shapes=[

time: 36.9 us -> 34.7 us (0.940)
  Pallas kernels: 35.4 us -> 34 us
  local copies, waits for them, and re-layouts: 1.35 us -> 0.61 us
    pallas_call x1, Pallas kernels: 35.4 us -> 34 us  [shards(): pl.pallas_call(functools.partial(layer_kernel, n), out_shape=pltpu.VMEM((...]
    unnamed x1, local copies, waits for them, and re-layouts: 1.35 us -> 0.61 us
where the time goes in v4:
time: 34.7 us; the launch traced here: 34.6 us
  Pallas kernels  34 us (98%)
  local copies, waits for them, and re-layouts  0.61 us (2%)
    pallas_call x1, Pallas kernels, shards(): pl.pallas_call(functools.partial(layer_kernel, n), out_shape=pltpu.VMEM((...  34 us

profile of v4, /device:TPU:1, one launch (start us, length us, event | category | flops | bytes accessed | tf_op | source)
XLA Modules:
  0.0 34.6 jit_solution(8791918042240961140)
XLA Ops:
  0.0 34.0 %shard_map.163 = bf16[8,1536]{1,0:T(8,128)(2,1)S(1)} custom-call(s32[4,16]{1,0:T(4,128)} %bitcast.10, s32[1024]{0:T(1024)} %lengths_h.1, s32[64]{0:T(128)} %owner_h.1, s32[4,8]{1,0:T(4,128)} %bitcast.11, bf16[16,1536]{1,0:T(8,128)(2,1)} %tokens_h.1, bf16[1536]{0:T(1024)(128)(2,1)} %gain_a_h.1, bf16[1536]{0:T(1024)(128)(2,1)} %gain_m_h.1, ...), custom_call_target="tpu_custom_call" | custom-call | tf_op jit(solution)/shard_map/pallas_call | solution.py:505
  34.0 0.6 %copy.19 = bf16[8,1536]{1,0:T(8,128)(2,1)} copy(bf16[8,1536]{1,0:T(8,128)(2,1)S(1)} %shard_map.163) | data formatting | bytes 49152

commit v5 on v3

--- a/solution.py
+++ b/solution.py
@@ -1,4 +1,5 @@
 import functools
+import itertools
 
 import jax
 import jax.numpy as jnp
@@ -102,6 +103,30 @@
     cols = width // hd
     inv_root = hd ** (-0.5)
 
+    side = round(n ** (1 / 3))
+    me_z, me_x, me_y = me // (side * side), lax.rem(me // side, side), lax.rem(me, side)
+    at_z = [lax.rem(me_z + d, side) * (side * side) for d in range(side)]
+    at_x = [lax.rem(me_x + d, side) * side for d in range(side)]
+    at_y = [lax.rem(me_y + d, side) for d in range(side)]
+
+    def hops(offset):
+        return sum(min(d, side - d) for d in offset)
+
+    offsets = sorted(
+        (o for o in itertools.product(range(side), repeat=3) if any(o)), key=lambda o: -hops(o)
+    )
+
+    def shifted(offset):
+        dz, dx, dy = offset
+        return at_z[dz] + at_x[dx] + at_y[dy]
+
+    sibling = {"kv": 1 - kv}
+    relocating = kv == 1
+    barrier = pltpu.get_barrier_semaphore()
+    for offset in offsets:
+        pl.semaphore_signal(barrier, 1, device_id={"req": shifted(offset)})
+    pl.semaphore_signal(barrier, 1, device_id=sibling)
+
     def load(src, dst, i):
         copy = pltpu.make_async_copy(src, dst, load_sems.at[i])
         copy.start()
@@ -115,16 +140,6 @@
     l_wk = load(wk_h, wqkv.at[:, pl.ds(qcols, hd)], 3)
     l_wv = load(wv_h, wqkv.at[:, pl.ds(qcols + hd, hd)], 4)
 
-    sibling = {"kv": 1 - kv}
-    relocating = kv == 1
-    barrier = pltpu.get_barrier_semaphore()
-
-    def greet(i, carry):
-        pl.semaphore_signal(barrier, 1, device_id={"req": lax.rem(me + i, n)})
-        return carry
-
-    pl.semaphore_signal(barrier, 1, device_id=sibling)
-    lax.fori_loop(1, n, greet, 0)
     l_ints = [
         load(src, dst, 13 + i)
         for i, (src, dst) in enumerate(
@@ -145,8 +160,8 @@
     l_wd = load(wd_h.at[0], wd.at[0], 11)
 
     def to_all(src_of, dst, phase):
-        def send(i, carry):
-            peer = lax.rem(me + i, n)
+        for offset in offsets:
+            peer = shifted(offset)
             pltpu.make_async_remote_copy(
                 src_ref=src_of(peer),
                 dst_ref=dst.at[me],
@@ -154,10 +169,7 @@
                 recv_sem=recv_sems.at[phase],
                 device_id={"req": peer},
             ).start()
-            return carry
-
         pltpu.make_async_copy(src_of(me), dst.at[me], recv_sems.at[phase]).start()
-        lax.fori_loop(1, n, send, 0)
 
     l_tok.wait()
     l_gain.wait()
@@ -184,18 +196,6 @@
     @pl.when(relocating)
     def _():
         to_all(lambda peer: t_out, t_in, 1)
-
-    swaps = []
-    for i, (src, dst) in enumerate(((wg_h, wg), (wu_h, wu), (wd_h, wd))):
-        swap = pltpu.make_async_remote_copy(
-            src_ref=src.at[0],
-            dst_ref=dst.at[1],
-            send_sem=w_send.at[i],
-            recv_sem=w_recv.at[i],
-            device_id=sibling,
-        )
-        swap.start()
-        swaps.append(swap)
 
     def attend(first, count):
         rows = slice(first * 8, (first + count) * 8)
@@ -304,6 +304,17 @@
             ]
     disp_out[...] = wide_a[...].reshape(experts, 2 * cols, hd).astype(BF)
     to_all(lambda peer: disp_out.at[peer // 2], disp_in, 2)
+    swaps = []
+    for i, (src, dst) in enumerate(((wg_h, wg), (wu_h, wu), (wd_h, wd))):
+        swap = pltpu.make_async_remote_copy(
+            src_ref=src.at[0],
+            dst_ref=dst.at[1],
+            send_sem=w_send.at[i],
+            recv_sem=w_recv.at[i],
+            device_id=sibling,
+        )
+        swap.start()
+        swaps.append(swap)
 
     wait_bytes(q_in, recv_sems.at[0])
     served = owner_s[me]
@@ -384,6 +395,17 @@
             [unpack(wide_b, lambda c: c * 2 + k, 2 * cols).astype(BF) for k in range(2)], axis=0
         )
 
+    owners = jnp.zeros((8, 128), jnp.int32)
+    owner_lane = lax.broadcasted_iota(jnp.int32, (8, 128), 1)
+    for c in range(n):
+        owners = jnp.where(owner_lane == c, owner_s[c], owners)
+    slot_row = lax.broadcasted_iota(jnp.int32, (n, n), 0)
+    moves = jnp.where(slot_row == owners[0:1, :n], 1.0, 0.0).astype(BF)
+
+    def find(c, found):
+        return jnp.where(owner_s[c] == me, c, found)
+
+    origin = lax.fori_loop(0, n, find, 0)
     l_wg.wait()
     l_wu.wait()
     l_wd.wait()
@@ -402,26 +424,20 @@
 
     @pl.when(relocating)
     def _():
-        owners = jnp.zeros((8, 128), jnp.int32)
-        owner_lane = lax.broadcasted_iota(jnp.int32, (8, 128), 1)
-        for c in range(n):
-            owners = jnp.where(owner_lane == c, owner_s[c], owners)
-        slot_row = lax.broadcasted_iota(jnp.int32, (n, n), 0)
-        moves = jnp.where(slot_row == owners[0:1, :n], 1.0, 0.0).astype(BF)
         wait_bytes(m_in, recv_sems.at[3])
         wide_m[...] = m_in[...].astype(F32).reshape(n * 16, hd)
         late_normed = rms_scaled(unpack(wide_m, lambda c: c, 16), gain_moe)
         ordered = jnp.dot(moves, late_normed, preferred_element_type=F32).astype(BF)
         late_result = run_expert(ordered)
 
-        def find(c, found):
-            return jnp.where(owner_s[c] == me, c, found)
-
-        origin = lax.fori_loop(0, n, find, 0)
         late_middle = jnp.concatenate(
             [wide_m[pl.ds(origin * 16 + c, 1), :] for c in range(cols)], axis=1
         )
         late_middle = jnp.broadcast_to(late_middle, (half, width))
+        for c in range(cols):
+            wide_m[pl.ds(c, n, stride=16), :] = late_result[:, c * hd : (c + 1) * hd]
+        late_out[...] = wide_m[...].reshape(n, 16, hd).astype(BF)
+        to_all(lambda peer: late_out.at[peer], late_in, 5)
         late_blend = in_parts(
             jnp.where(
                 lane < n,
@@ -429,10 +445,6 @@
                 0.0,
             )[:, :n]
         )
-        for c in range(cols):
-            wide_m[pl.ds(c, n, stride=16), :] = late_result[:, c * hd : (c + 1) * hd]
-        late_out[...] = wide_m[...].reshape(n, 16, hd).astype(BF)
-        to_all(lambda peer: late_out.at[peer], late_in, 5)
         wait_bytes(late_in, recv_sems.at[5])
         wide_m[...] = late_in[...].astype(F32).reshape(n * 16, hd)
         late = late_middle + blended(late_blend, unpack(wide_m, lambda c: c, 16).astype(BF))
@@ -493,7 +505,7 @@
         dma = pltpu.SemaphoreType.DMA
         return pl.pallas_call(
             functools.partial(layer_kernel, n),
-            out_shape=jax.ShapeDtypeStruct((half, width), BF),
+            out_shape=pltpu.VMEM((half, width), BF),
             in_specs=[hbm] * 4 + [hbm] * 13,
             out_specs=pl.BlockSpec(memory_space=pltpu.VMEM),
             scratch_shapes=[

time: 36.9 us -> 33.9 us (0.919)
  Pallas kernels: 35.4 us -> 33.1 us
  local copies, waits for them, and re-layouts: 1.35 us -> 0.61 us
    pallas_call x1, Pallas kernels: 35.4 us -> 33.1 us  [shards(): pl.pallas_call(functools.partial(layer_kernel, n), out_shape=pltpu.VMEM((...]
    unnamed x1, local copies, waits for them, and re-layouts: 1.35 us -> 0.61 us
where the time goes in v5:
time: 33.9 us; the launch traced here: 33.8 us
  Pallas kernels  33.1 us (98%)
  local copies, waits for them, and re-layouts  0.61 us (2%)
    pallas_call x1, Pallas kernels, shards(): pl.pallas_call(functools.partial(layer_kernel, n), out_shape=pltpu.VMEM((...  33.1 us

profile of v5, /device:TPU:1, one launch (start us, length us, event | category | flops | bytes accessed | tf_op | source)
XLA Modules:
  0.0 33.8 jit_solution(974590029071273845)
XLA Ops:
  0.0 33.1 %shard_map.163 = bf16[8,1536]{1,0:T(8,128)(2,1)S(1)} custom-call(s32[4,16]{1,0:T(4,128)} %bitcast.10, s32[1024]{0:T(1024)} %lengths_h.1, s32[64]{0:T(128)} %owner_h.1, s32[4,8]{1,0:T(4,128)} %bitcast.11, bf16[16,1536]{1,0:T(8,128)(2,1)} %tokens_h.1, bf16[1536]{0:T(1024)(128)(2,1)} %gain_a_h.1, bf16[1536]{0:T(1024)(128)(2,1)} %gain_m_h.1, ...), custom_call_target="tpu_custom_call" | custom-call | tf_op jit(solution)/shard_map/pallas_call | solution.py:506
  33.2 0.6 %copy.19 = bf16[8,1536]{1,0:T(8,128)(2,1)} copy(bf16[8,1536]{1,0:T(8,128)(2,1)S(1)} %shard_map.163) | data formatting | bytes 49152

commit v6 on v5

--- a/solution.py
+++ b/solution.py
@@ -105,9 +105,10 @@
 
     side = round(n ** (1 / 3))
     me_z, me_x, me_y = me // (side * side), lax.rem(me // side, side), lax.rem(me, side)
-    at_z = [lax.rem(me_z + d, side) * (side * side) for d in range(side)]
-    at_x = [lax.rem(me_x + d, side) * side for d in range(side)]
-    at_y = [lax.rem(me_y + d, side) for d in range(side)]
+    turn = 1 + (side - 2) * kv
+    at_z = [lax.rem(me_z + d * turn, side) * (side * side) for d in range(side)]
+    at_x = [lax.rem(me_x + d * turn, side) * side for d in range(side)]
+    at_y = [lax.rem(me_y + d * turn, side) for d in range(side)]
 
     def hops(offset):
         return sum(min(d, side - d) for d in offset)

time: 33.9 us -> 33.5 us (0.988)
  no operation moved by 1% of the time
where the time goes in v6:
time: 33.5 us; the launch traced here: 33.4 us
  Pallas kernels  32.8 us (98%)
  local copies, waits for them, and re-layouts  0.61 us (2%)
    pallas_call x1, Pallas kernels, shards(): pl.pallas_call(functools.partial(layer_kernel, n), out_shape=pltpu.VMEM((...  32.8 us

profile of v6, /device:TPU:1, one launch (start us, length us, event | category | flops | bytes accessed | tf_op | source)
XLA Modules:
  0.0 33.4 jit_solution(8564627662310232406)
XLA Ops:
  0.0 32.8 %shard_map.163 = bf16[8,1536]{1,0:T(8,128)(2,1)S(1)} custom-call(s32[4,16]{1,0:T(4,128)} %bitcast.10, s32[1024]{0:T(1024)} %lengths_h.1, s32[64]{0:T(128)} %owner_h.1, s32[4,8]{1,0:T(4,128)} %bitcast.11, bf16[16,1536]{1,0:T(8,128)(2,1)} %tokens_h.1, bf16[1536]{0:T(1024)(128)(2,1)} %gain_a_h.1, bf16[1536]{0:T(1024)(128)(2,1)} %gain_m_h.1, ...), custom_call_target="tpu_custom_call" | custom-call | tf_op jit(solution)/shard_map/pallas_call | solution.py:507
  32.8 0.6 %copy.19 = bf16[8,1536]{1,0:T(8,128)(2,1)} copy(bf16[8,1536]{1,0:T(8,128)(2,1)S(1)} %shard_map.163) | data formatting | bytes 49152

commit v7 on v6

--- a/solution.py
+++ b/solution.py
@@ -70,7 +70,9 @@
     lengths_s,
     owner_s,
     routes_s,
-    fin,
+    mid_late,
+    early_mix,
+    late_mix,
     row_sum,
     row_in,
     t_out,
@@ -360,11 +362,33 @@
         part_c = blend - part_a - part_b
         return jnp.concatenate([part_a, part_b, part_c], axis=0).astype(BF)
 
-    def blended(parts, rows):
-        mixed = jnp.dot(parts, rows, preferred_element_type=F32)
-        return mixed[:half] + mixed[half : 2 * half] + mixed[2 * half :]
-
     blend_parts = in_parts(route_weights(normed_two, early) * peer_place)
+
+    def spread(parts, mix, block):
+        count = parts.shape[0]
+        span = n * block
+        at = lax.broadcasted_iota(jnp.int32, (1, span), 1)
+        owner_of = (at * (65536 // block + 1)) // 65536
+        within = at - owner_of * block
+        per_col = block // cols
+        wanted = owner_of + (within % per_col) * n
+        pick_lane = lax.broadcasted_iota(jnp.int32, (parts.shape[1], span), 0) == wanted
+        wide = jnp.dot(
+            parts, jnp.where(pick_lane, 1.0, 0.0).astype(BF), preferred_element_type=F32
+        )
+        for c in range(cols):
+            mix[c * count : (c + 1) * count, :] = jnp.where(
+                within // per_col == c, wide, 0.0
+            ).astype(BF)
+
+    def gathered(mix, arrived_rows):
+        block = arrived_rows.shape[1]
+        flat = arrived_rows[...].astype(F32).reshape(n * block, hd).astype(BF)
+        sums = jnp.dot(mix[...], flat, preferred_element_type=F32)
+        thirds = [sums[i * half : (i + 1) * half] for i in range(3 * cols)]
+        return jnp.concatenate(
+            [thirds[3 * c] + thirds[3 * c + 1] + thirds[3 * c + 2] for c in range(cols)], axis=1
+        )
 
     @pl.when(relocating)
     def _():
@@ -407,6 +431,7 @@
         return jnp.where(owner_s[c] == me, c, found)
 
     origin = lax.fori_loop(0, n, find, 0)
+    spread(blend_parts, early_mix, 2 * cols)
     l_wg.wait()
     l_wu.wait()
     l_wd.wait()
@@ -446,16 +471,18 @@
                 0.0,
             )[:, :n]
         )
+        mid_late[...] = late_middle
+        spread(late_blend, late_mix, 16)
+
+    @pl.when(relocating)
+    def _():
         wait_bytes(late_in, recv_sems.at[5])
-        wide_m[...] = late_in[...].astype(F32).reshape(n * 16, hd)
-        late = late_middle + blended(late_blend, unpack(wide_m, lambda c: c, 16).astype(BF))
-        fin[half - 1 : half, :] = late[half - 1 : half, :]
 
     wait_bytes(ret_in, recv_sems.at[4])
-    wide_b[...] = ret_in[...].astype(F32).reshape(n * 2 * cols, hd)
-    done = middle + blended(blend_parts, unpack_pair())
+    done = middle + gathered(early_mix, ret_in)
+    late = mid_late[...] + gathered(late_mix, late_in)
     kept = (lax.broadcasted_iota(jnp.int32, (half, width), 0) == half - 1) & relocating
-    out_ref[...] = jnp.where(kept, fin[...], done).astype(BF)
+    out_ref[...] = jnp.where(kept, late, done).astype(BF)
 
     cross.wait_send()
     for swap in swaps:
@@ -539,6 +566,8 @@
                 pltpu.SMEM(new_owner.shape, jnp.int32),
                 pltpu.SMEM(routes.shape[::-1], jnp.int32),
                 pltpu.VMEM((half, width), F32),
+                pltpu.VMEM((3 * half * cols, n * 2 * cols), BF),
+                pltpu.VMEM((3 * half * cols, n * 16), BF),
                 pltpu.VMEM((1, width), F32),
                 pltpu.VMEM((1, width), F32),
                 pltpu.VMEM((16, hd), BF),

time: 33.5 us -> 33.5 us (level)
  no operation moved by 1% of the time
where the time goes in v7:
time: 33.5 us; the launch traced here: 33.4 us
  Pallas kernels  32.8 us (98%)
  local copies, waits for them, and re-layouts  0.61 us (2%)
    pallas_call x1, Pallas kernels, shards(): pl.pallas_call(functools.partial(layer_kernel, n), out_shape=pltpu.VMEM((...  32.8 us

profile of v7, /device:TPU:1, one launch (start us, length us, event | category | flops | bytes accessed | tf_op | source)
XLA Modules:
  0.0 33.4 jit_solution(4408249123636308217)
XLA Ops:
  0.0 32.8 %shard_map.163 = bf16[8,1536]{1,0:T(8,128)(2,1)S(1)} custom-call(s32[4,16]{1,0:T(4,128)} %bitcast.10, s32[1024]{0:T(1024)} %lengths_h.1, s32[64]{0:T(128)} %owner_h.1, s32[4,8]{1,0:T(4,128)} %bitcast.11, bf16[16,1536]{1,0:T(8,128)(2,1)} %tokens_h.1, bf16[1536]{0:T(1024)(128)(2,1)} %gain_a_h.1, bf16[1536]{0:T(1024)(128)(2,1)} %gain_m_h.1, ...), custom_call_target="tpu_custom_call" | custom-call | tf_op jit(solution)/shard_map/pallas_call | solution.py:534
  32.8 0.6 %copy.19 = bf16[8,1536]{1,0:T(8,128)(2,1)} copy(bf16[8,1536]{1,0:T(8,128)(2,1)S(1)} %shard_map.163) | data formatting | bytes 49152

commit v8 on v6

--- a/solution.py
+++ b/solution.py
@@ -114,7 +114,7 @@
         return sum(min(d, side - d) for d in offset)
 
     offsets = sorted(
-        (o for o in itertools.product(range(side), repeat=3) if any(o)), key=lambda o: -hops(o)
+        (o for o in itertools.product(range(side), repeat=3) if any(o)), key=lambda o: (-hops(o), o[::-1])
     )
 
     def shifted(offset):

time: 33.5 us -> 33.3 us (level)
  no operation moved by 1% of the time
where the time goes in v8:
time: 33.3 us; the launch traced here: 33.2 us
  Pallas kernels  32.6 us (98%)
  local copies, waits for them, and re-layouts  0.61 us (2%)
    pallas_call x1, Pallas kernels, shards(): pl.pallas_call(functools.partial(layer_kernel, n), out_shape=pltpu.VMEM((...  32.6 us

profile of v8, /device:TPU:1, one launch (start us, length us, event | category | flops | bytes accessed | tf_op | source)
XLA Modules:
  0.0 33.2 jit_solution(15407011271297822912)
XLA Ops:
  0.0 32.6 %shard_map.163 = bf16[8,1536]{1,0:T(8,128)(2,1)S(1)} custom-call(s32[4,16]{1,0:T(4,128)} %bitcast.10, s32[1024]{0:T(1024)} %lengths_h.1, s32[64]{0:T(128)} %owner_h.1, s32[4,8]{1,0:T(4,128)} %bitcast.11, bf16[16,1536]{1,0:T(8,128)(2,1)} %tokens_h.1, bf16[1536]{0:T(1024)(128)(2,1)} %gain_a_h.1, bf16[1536]{0:T(1024)(128)(2,1)} %gain_m_h.1, ...), custom_call_target="tpu_custom_call" | custom-call | tf_op jit(solution)/shard_map/pallas_call | solution.py:507
  32.6 0.6 %copy.19 = bf16[8,1536]{1,0:T(8,128)(2,1)} copy(bf16[8,1536]{1,0:T(8,128)(2,1)S(1)} %shard_map.163) | data formatting | bytes 49152
